TPU v7x, 32 devices: a whole 2x2x4 slice. The times are simulated.
32 devices in a mesh: dp: 8 (over z, x), fsdp: 4 (over y, core).
Axes of the slice: x: 2, y: 2, z: 4, core: 2. Of those that a mesh axis runs over, the one named last changes fastest.
Arguments:
- tokens: bfloat16 [12288, 1280], P(('dp', 'fsdp')), may hold values from -6 to 6
- teacher: bfloat16 [12288, 1280], P(('dp', 'fsdp')), may hold values from -6 to 6
- picture: int32 [12288], P(('dp', 'fsdp')), may hold values from 0 to 767, as said below
- places: int32 [12288, 2], P(('dp', 'fsdp')), may hold values from 0 to 15, as said below
- validity: int32 [12288], P(('dp', 'fsdp')), may hold values from 0 to 1, as said below
- first_gain: bfloat16 [1280], P('dp'), may hold values from 0.5 to 1.5
- first_shift: bfloat16 [1280], P('dp'), may hold values from -1.5 to 1.5
- mixer_weight: bfloat16 [1280, 3, 1280], P('dp', None, 'fsdp'), may hold values from -0.15625 to 0.15625
- mixer_bias: bfloat16 [3840], P('dp'), may hold values from -1.5 to 1.5
- output_weight: bfloat16 [1280, 1280], P('fsdp', 'dp'), may hold values from -0.625 to 0.625
- output_bias: bfloat16 [1280], P('dp'), may hold values from -1.5 to 1.5
- second_gain: bfloat16 [1280], P('dp'), may hold values from 0.5 to 1.5
- second_shift: bfloat16 [1280], P('dp'), may hold values from -1.5 to 1.5
- upward_weight: bfloat16 [1280, 5120], P('dp', 'fsdp'), may hold values from -0.15625 to 0.15625
- upward_bias: bfloat16 [5120], P('dp'), may hold values from -1.5 to 1.5
- downward_weight: bfloat16 [5120, 1280], P('fsdp', 'dp'), may hold values from -0.125 to 0.125
- downward_bias: bfloat16 [1280], P('dp'), may hold values from -1.5 to 1.5
Outputs:
- result: bfloat16 [12288, 1280], P(('dp', 'fsdp'))
- loss: float32 [], replicated
- grad_tokens: float32 [12288, 1280], P(('dp', 'fsdp'))
- grad_first_gain: float32 [1280], P('dp')
- grad_first_shift: float32 [1280], P('dp')
- grad_mixer_weight: float32 [1280, 3, 1280], P('dp', None, 'fsdp')
- grad_mixer_bias: float32 [2560], P('dp')
- grad_value_bias: float32 [1280], P('dp')
- grad_output_weight: float32 [1280, 1280], P('fsdp', 'dp')
- grad_output_bias: float32 [1280], P('dp')
- grad_second_gain: float32 [1280], P('dp')
- grad_second_shift: float32 [1280], P('dp')
- grad_upward_weight: float32 [1280, 5120], P('dp', 'fsdp')
- grad_upward_bias: float32 [5120], P('dp')
- grad_downward_weight: float32 [5120, 1280], P('fsdp', 'dp')
- grad_downward_bias: float32 [1280], P('dp')
Inputs may be any that keep to these rules, and one draw needn't show every extreme that they name: Pictures never span rows; along a row the picture numbers never fall, each picture holds 16 to 64 patches except the one that the row's end cuts. A patch's places are its row and column in a picture of 4 to 16 columns, filled row by row; rows stay under 64 // 4 + 1. `validity`: padding only ends a row; every row has real patches.
All inputs are finite; a program needn't handle non-finite values.
Results may differ from a plain program's by a relative error of at most 0.014.
Values may be sent and summed in bfloat16 or wider, within the bound.
A program may use at most 192 MiB of HBM per device.

v0:
```python
import jax
import jax.numpy as jnp
from jax import lax
from jax.sharding import PartitionSpec as P

D = 1280
HD = 80
FF = 5120
ROW_PATCHES = 128
MB = 3


EPSILON = 1e-06


def norm_forward(values, scaler, offset):
    average = jnp.mean(values, axis=-1, keepdims=True)
    centered = values - average
    reciprocal = lax.rsqrt(jnp.mean(centered * centered, axis=-1, keepdims=True) + EPSILON)
    normed = centered * reciprocal
    return (normed * scaler.astype(jnp.float32) + offset.astype(jnp.float32), normed, reciprocal)


def norm_backward(gradient, normed, reciprocal, scaler):
    scaled = gradient * scaler.astype(jnp.float32)
    adjusted = (
        scaled
        - jnp.mean(scaled, axis=-1, keepdims=True)
        - normed * jnp.mean(scaled * normed, axis=-1, keepdims=True)
    )
    return (adjusted * reciprocal, jnp.sum(gradient * normed, axis=0), jnp.sum(gradient, axis=0))


def tables(places):
    quarter = HD // 4
    frequency = 1.0 / 10000.0 ** (jnp.arange(quarter, dtype=jnp.float32) * 4.0 / HD)
    row_angle = places[:, 0:1].astype(jnp.float32) * frequency
    col_angle = places[:, 1:2].astype(jnp.float32) * frequency
    angle_all = jnp.concatenate([row_angle, col_angle, row_angle, col_angle], axis=-1)
    return (jnp.cos(angle_all)[:, None, :], jnp.sin(angle_all)[:, None, :])


def rotate(values, cosine, sine):
    halfway = HD // 2
    flipped = jnp.concatenate([-values[..., halfway:], values[..., :halfway]], axis=-1)
    return values * cosine + flipped * sine


def unrotate(gradient, cosine, sine):
    halfway = HD // 2
    shifted = gradient * sine
    return gradient * cosine + jnp.concatenate(
        [shifted[..., halfway:], -shifted[..., :halfway]], axis=-1
    )


def allowed_mask(picture, validity):
    picture_rows = picture.reshape(-1, ROW_PATCHES)
    occupancy_flags = validity.reshape(-1, ROW_PATCHES) > 0
    shared_picture_mask = picture_rows[:, :, None] == picture_rows[:, None, :]
    self_pairs = jnp.eye(ROW_PATCHES, dtype=bool)[None]
    return (shared_picture_mask & occupancy_flags[:, None, :] | self_pairs)[:, None]


def scores_of(query, key_rows, permitted_pairs):
    products = jnp.einsum(
        "bqhd,bkhd->bhqk", query, key_rows, preferred_element_type=jnp.float32
    ) * HD ** (-0.5)
    return jnp.where(permitted_pairs, products, -1e30)


def attend(query, key_rows, value_rows, permitted_pairs):
    scores = scores_of(query, key_rows, permitted_pairs)
    maximum = jnp.max(scores, axis=-1, keepdims=True)
    log_total = maximum + jnp.log(jnp.sum(jnp.exp(scores - maximum), axis=-1, keepdims=True))
    probs = jnp.exp(scores - log_total).astype(jnp.bfloat16)
    attended = jnp.einsum("bhqk,bkhd->bqhd", probs, value_rows, preferred_element_type=jnp.float32)
    return (attended, log_total)


def attend_back(grad_attended, query, key_rows, value_rows, permitted_pairs, log_total):
    scores = scores_of(query, key_rows, permitted_pairs)
    probs = jnp.exp(scores - log_total)
    grad_probs = jnp.einsum(
        "bqhd,bkhd->bhqk", grad_attended, value_rows, preferred_element_type=jnp.float32
    )
    delta = jnp.sum(grad_probs * probs, axis=-1, keepdims=True)
    grad_scores = (probs * (grad_probs - delta)).astype(jnp.bfloat16)
    scaling = HD ** (-0.5)
    grad_query = (
        jnp.einsum("bhqk,bkhd->bqhd", grad_scores, key_rows, preferred_element_type=jnp.float32)
        * scaling
    )
    grad_key = (
        jnp.einsum("bhqk,bqhd->bkhd", grad_scores, query, preferred_element_type=jnp.float32)
        * scaling
    )
    grad_value = jnp.einsum(
        "bhqk,bqhd->bkhd",
        probs.astype(jnp.bfloat16),
        grad_attended,
        preferred_element_type=jnp.float32,
    )
    return (grad_query, grad_key, grad_value)


def quick_gelu_grad(grad_active, upper):
    sigmoid_up = jax.nn.sigmoid(1.702 * upper)
    return (grad_active * (sigmoid_up + 1.702 * upper * sigmoid_up * (1.0 - sigmoid_up))).astype(
        jnp.bfloat16
    )


def own_slice(vector, data_index, data_ways):
    length = vector.shape[0] // data_ways
    return lax.dynamic_slice_in_dim(vector, data_index * length, length, 0)


def on_device(
    tokens,
    teacher,
    picture,
    places,
    validity,
    first_gain,
    first_shift,
    mixer_weight,
    mixer_bias,
    output_weight,
    output_bias,
    second_gain,
    second_shift,
    upward_weight,
    upward_bias,
    downward_weight,
    downward_bias,
):
    data_ways = lax.axis_size("dp")
    split_ways = lax.axis_size("fsdp")
    member = lax.axis_index("fsdp")
    data_index = lax.axis_index("dp")
    occupancy_flags = validity.astype(jnp.float32)
    token_tally = lax.psum(jnp.sum(occupancy_flags), ("dp", "fsdp"))
    factor = tokens.shape[0] * data_ways * split_ways / token_tally
    (
        mixer_local,
        output_local,
        upward_local,
        downward_local,
        gain_one,
        shift_one,
        mixer_shift,
        output_shift,
        gain_two,
        shift_two,
        upward_shift,
        downward_shift,
    ) = (
        lax.all_gather(mixer_weight, "dp", axis=0, tiled=True),
        lax.all_gather(output_weight, "dp", axis=1, tiled=True),
        lax.all_gather(upward_weight, "dp", axis=0, tiled=True),
        lax.all_gather(downward_weight, "dp", axis=1, tiled=True),
        lax.all_gather(first_gain, "dp", axis=0, tiled=True),
        lax.all_gather(first_shift, "dp", axis=0, tiled=True),
        lax.all_gather(mixer_bias, "dp", axis=0, tiled=True),
        lax.all_gather(output_bias, "dp", axis=0, tiled=True),
        lax.all_gather(second_gain, "dp", axis=0, tiled=True),
        lax.all_gather(second_shift, "dp", axis=0, tiled=True),
        lax.all_gather(upward_bias, "dp", axis=0, tiled=True),
        lax.all_gather(downward_bias, "dp", axis=0, tiled=True),
    )
    width_local = output_local.shape[0]
    heads_local = width_local // HD
    hidden_local = upward_local.shape[1]
    mixer_flat = mixer_local.reshape(D, 3 * width_local)
    mixer_piece = lax.dynamic_slice_in_dim(
        mixer_shift.reshape(3, D), member * width_local, width_local, 1
    )
    mixer_piece = mixer_piece.reshape(3 * width_local).astype(jnp.float32)
    upward_piece = lax.dynamic_slice_in_dim(
        upward_shift, member * hidden_local, hidden_local, 0
    ).astype(jnp.float32)
    packed_rows = tokens.shape[0] // MB
    errors = jnp.zeros((), jnp.float32)
    matrix_sums = None
    small_sums = None
    results = []
    input_grads = []
    for micro in range(MB):
        start_offset = micro * packed_rows
        inputs = tokens[start_offset : start_offset + packed_rows].astype(jnp.float32)
        target = teacher[start_offset : start_offset + packed_rows].astype(jnp.float32)
        occupied_rows = occupancy_flags[start_offset : start_offset + packed_rows]
        picture_rows = picture[start_offset : start_offset + packed_rows]
        local_picture = (picture_rows - picture_rows[0]).astype(jnp.bfloat16)
        place_rows = places[start_offset : start_offset + packed_rows].astype(jnp.bfloat16)
        live_marks = validity[start_offset : start_offset + packed_rows].astype(jnp.bfloat16)
        shifted_one, normed_one, recip_one = norm_forward(inputs, gain_one, shift_one)
        lowered_one = shifted_one.astype(jnp.bfloat16)
        group_one, group_picture, group_places, group_live = (
            lax.all_gather(lowered_one, "fsdp", axis=0, tiled=True),
            lax.all_gather(local_picture, "fsdp", axis=0, tiled=True),
            lax.all_gather(place_rows, "fsdp", axis=0, tiled=True),
            lax.all_gather(live_marks, "fsdp", axis=0, tiled=True),
        )
        group_rows = group_one.shape[0]
        mixed = jnp.dot(group_one, mixer_flat, preferred_element_type=jnp.float32) + mixer_piece
        mixed = mixed.reshape(group_rows, 3, heads_local, HD)
        cosine, sine = tables(group_places)
        query = (
            rotate(mixed[:, 0], cosine, sine)
            .astype(jnp.bfloat16)
            .reshape(-1, ROW_PATCHES, heads_local, HD)
        )
        key_rows = (
            rotate(mixed[:, 1], cosine, sine)
            .astype(jnp.bfloat16)
            .reshape(-1, ROW_PATCHES, heads_local, HD)
        )
        value_rows = mixed[:, 2].astype(jnp.bfloat16).reshape(-1, ROW_PATCHES, heads_local, HD)
        permitted_pairs = allowed_mask(group_picture, group_live)
        attended, log_total = attend(query, key_rows, value_rows, permitted_pairs)
        attended = attended.reshape(group_rows, width_local).astype(jnp.bfloat16)
        branch = lax.psum_scatter(
            jnp.dot(attended, output_local, preferred_element_type=jnp.float32).astype(
                jnp.bfloat16
            ),
            "fsdp",
            scatter_dimension=0,
            tiled=True,
        ).astype(jnp.float32)
        middle = inputs + branch + output_shift.astype(jnp.float32)
        shifted_two, normed_two, recip_two = norm_forward(middle, gain_two, shift_two)
        lowered_two = shifted_two.astype(jnp.bfloat16)
        group_two = lax.all_gather(lowered_two, "fsdp", axis=0, tiled=True)
        upper = jnp.dot(group_two, upward_local, preferred_element_type=jnp.float32) + upward_piece
        active = (upper * jax.nn.sigmoid(1.702 * upper)).astype(jnp.bfloat16)
        lowered = lax.psum_scatter(
            jnp.dot(active, downward_local, preferred_element_type=jnp.float32).astype(
                jnp.bfloat16
            ),
            "fsdp",
            scatter_dimension=0,
            tiled=True,
        ).astype(jnp.float32)
        outputs = middle + lowered + downward_shift.astype(jnp.float32)
        difference = outputs - target
        masked = occupied_rows[:, None] * difference
        errors = errors + jnp.sum(masked * difference)
        grad_out = 2.0 * factor * masked
        grad_low = grad_out.astype(jnp.bfloat16)
        down_bias_term = jnp.sum(grad_low.astype(jnp.float32), axis=0)
        group_grad = lax.all_gather(grad_low, "fsdp", axis=0, tiled=True)
        g_down = jnp.einsum("rf,rd->fd", active, group_grad, preferred_element_type=jnp.float32)
        grad_active = jnp.einsum(
            "rd,fd->rf", group_grad, downward_local, preferred_element_type=jnp.float32
        )
        grad_upper = quick_gelu_grad(grad_active, upper)
        g_up = jnp.einsum("rd,rf->df", group_two, grad_upper, preferred_element_type=jnp.float32)
        up_bias_term = lax.dynamic_update_slice_in_dim(
            jnp.zeros((FF,), jnp.float32),
            jnp.sum(grad_upper.astype(jnp.float32), axis=0),
            member * hidden_local,
            0,
        )
        grad_two = lax.psum_scatter(
            jnp.einsum(
                "rf,df->rd", grad_upper, upward_local, preferred_element_type=jnp.float32
            ).astype(jnp.bfloat16),
            "fsdp",
            scatter_dimension=0,
            tiled=True,
        ).astype(jnp.float32)
        back_two, g_gain_two, g_shift_two = norm_backward(grad_two, normed_two, recip_two, gain_two)
        grad_middle = grad_out + back_two
        grad_branch = grad_middle.astype(jnp.bfloat16)
        out_bias_term = jnp.sum(grad_branch.astype(jnp.float32), axis=0)
        group_branch = lax.all_gather(grad_branch, "fsdp", axis=0, tiled=True)
        g_output = jnp.einsum(
            "rd,re->de", attended, group_branch, preferred_element_type=jnp.float32
        )
        grad_attended = jnp.einsum(
            "re,de->rd", group_branch, output_local, preferred_element_type=jnp.float32
        )
        grad_attended = grad_attended.astype(jnp.bfloat16).reshape(-1, ROW_PATCHES, heads_local, HD)
        grad_query, grad_key, grad_value = attend_back(
            grad_attended, query, key_rows, value_rows, permitted_pairs, log_total
        )
        grad_mixed = jnp.stack(
            [
                unrotate(grad_query.reshape(group_rows, heads_local, HD), cosine, sine),
                unrotate(grad_key.reshape(group_rows, heads_local, HD), cosine, sine),
                grad_value.reshape(group_rows, heads_local, HD),
            ],
            axis=1,
        )
        grad_mixed = grad_mixed.reshape(group_rows, 3 * width_local).astype(jnp.bfloat16)
        g_mixer = jnp.einsum("rd,re->de", group_one, grad_mixed, preferred_element_type=jnp.float32)
        g_mixer = g_mixer.reshape(D, 3, width_local)
        mixer_bias_term = lax.dynamic_update_slice_in_dim(
            jnp.zeros((3, D), jnp.float32),
            jnp.sum(grad_mixed.astype(jnp.float32), axis=0).reshape(3, width_local),
            member * width_local,
            1,
        )
        mixer_bias_term = mixer_bias_term.reshape(3 * D)
        grad_one = lax.psum_scatter(
            jnp.einsum(
                "re,de->rd", grad_mixed, mixer_flat, preferred_element_type=jnp.float32
            ).astype(jnp.bfloat16),
            "fsdp",
            scatter_dimension=0,
            tiled=True,
        ).astype(jnp.float32)
        back_one, g_gain_one, g_shift_one = norm_backward(grad_one, normed_one, recip_one, gain_one)
        grad_inputs = grad_middle + back_one
        matrices = (g_mixer, g_output, g_up, g_down)
        smalls = (
            g_gain_one,
            g_shift_one,
            mixer_bias_term,
            out_bias_term,
            g_gain_two,
            g_shift_two,
            up_bias_term,
            down_bias_term,
        )
        matrix_sums = (
            matrices if matrix_sums is None else jax.tree.map(jnp.add, matrix_sums, matrices)
        )
        small_sums = smalls if small_sums is None else jax.tree.map(jnp.add, small_sums, smalls)
        results.append(outputs.astype(jnp.bfloat16))
        input_grads.append(grad_inputs)
    g_mixer_sum, g_output_sum, g_up_sum, g_down_sum = matrix_sums
    reduced = (
        lax.psum_scatter(
            g_mixer_sum.astype(jnp.bfloat16), "dp", scatter_dimension=0, tiled=True
        ).astype(jnp.float32),
        lax.psum_scatter(
            g_output_sum.astype(jnp.bfloat16), "dp", scatter_dimension=1, tiled=True
        ).astype(jnp.float32),
        lax.psum_scatter(
            g_up_sum.astype(jnp.bfloat16), "dp", scatter_dimension=0, tiled=True
        ).astype(jnp.float32),
        lax.psum_scatter(
            g_down_sum.astype(jnp.bfloat16), "dp", scatter_dimension=1, tiled=True
        ).astype(jnp.float32),
    )
    totals = lax.psum(
        (
            small_sums[0],
            small_sums[1],
            small_sums[2],
            small_sums[3],
            small_sums[4],
            small_sums[5],
            small_sums[6],
            small_sums[7],
            errors,
        ),
        ("dp", "fsdp"),
    )
    pieces = [own_slice(totals[index], data_index, data_ways) for index in range(8)]
    query_key_piece = own_slice(totals[2][: 2 * D], data_index, data_ways)
    value_piece = own_slice(totals[2][2 * D :], data_index, data_ways)
    loss = totals[8] / (token_tally * D)
    return (
        jnp.concatenate(results, axis=0),
        loss,
        jnp.concatenate(input_grads, axis=0),
        pieces[0],
        pieces[1],
        reduced[0],
        query_key_piece,
        value_piece,
        reduced[1],
        pieces[3],
        pieces[4],
        pieces[5],
        reduced[2],
        pieces[6],
        reduced[3],
        pieces[7],
    )


def solution(mesh):
    return jax.shard_map(
        on_device,
        mesh=mesh,
        in_specs=(
            P(("dp", "fsdp"), None),
            P(("dp", "fsdp"), None),
            P(("dp", "fsdp")),
            P(("dp", "fsdp"), None),
            P(("dp", "fsdp")),
            P("dp"),
            P("dp"),
            P("dp", None, "fsdp"),
            P("dp"),
            P("fsdp", "dp"),
            P("dp"),
            P("dp"),
            P("dp"),
            P("dp", "fsdp"),
            P("dp"),
            P("fsdp", "dp"),
            P("dp"),
        ),
        out_specs=(
            P(("dp", "fsdp"), None),
            P(),
            P(("dp", "fsdp"), None),
            P("dp"),
            P("dp"),
            P("dp", None, "fsdp"),
            P("dp"),
            P("dp"),
            P("fsdp", "dp"),
            P("dp"),
            P("dp"),
            P("dp"),
            P("dp", "fsdp"),
            P("dp"),
            P("fsdp", "dp"),
            P("dp"),
        ),
        check_vma=False,
    )
```

profile of v0, /device:TPU:0, one launch (start us, length us, event | category | flops | bytes accessed | tf_op | source)
XLA Modules:
  0.0 1211.5 jit_solution(69246918830144462)
XLA Ops:
  16.6 40.7 %all-reduce.9 = (bf16[1280]{0:T(1024)(128)(2,1)}, bf16[1280]{0:T(1024)(128)(2,1)}, bf16[1280]{0:T(1024)(128)(2,1)}, bf16[1280]{0:T(1024)(128)(2,1)}, bf16[1280]{...) all-reduce(bf16[1280]{0:T(1024)(128)(2,1)S(1)} %dynamic-update-slic, ...), channel_id=1, replica_groups=mesh['dp'=8,'fsdp'=4] {'dp'}, use_global_device_ids=true, to_apply=%add.6 | all-reduce | flops 11520 | bytes 46080
  63.2 5.0 all-gather.6
  70.7 5.0 all-gather.5
  75.7 5.0 all-gather.4
  80.8 5.0 all-gather.3
  85.8 5.0 all-gather.1
  90.9 5.0 all-gather
  95.9 5.0 all_gather.124
  101.0 5.0 all_gather.106
  106.0 5.0 all_gather.119
  115.1 32.7 %all_gather.107 = bf16[320,1280]{0,1:T(8,128)(2,1)S(1)} all-gather(bf16[320,160]{0,1:T(8,128)(2,1)S(1)} %copy-done.76), channel_id=1, replica_groups=mesh['dp'=8,'fsdp'=4] {'dp'}, dimensions={1}, use_global_device_ids=true | all-gather | bytes 921600 | tf_op jit(solution)/shard_map/all_gather | solution.py:160
  147.8 5.6 copy.112
  153.6 3.6 convolution_add_fusion.11
  171.3 23.9 %reduce-scatter.17.cloned.1.call-done = bf16[128,1280]{1,0:T(8,128)(2,1)} async-done(((bf16[512,1280]{1,0:T(8,128)(2,1)}), bf16[128,1280]{1,0:T(8,128)(2,1)}) %reduce-scatter.17.cloned.1.call-update) | async-done | bytes 327696 | tf_op jit(solution)/shard_map/reduce_scatter | solution.py:224
  198.3 3.6 fusion.172
  202.2 14.4 %all-gather.33.cloned.1.call-done = bf16[512,1280]{1,0:T(8,128)(2,1)} async-done(((bf16[128,1280]{1,0:T(8,128)(2,1)}), bf16[512,1280]{1,0:T(8,128)(2,1)}) %all-gather.33.cloned.1.call-update) | async-done | bytes 1310736 | tf_op jit(solution)/shard_map/all_gather | solution.py:201
  216.6 3.6 convolution_add_fusion.10
  240.4 3.6 convolution_add_fusion.9
  272.5 25.7 %reduce-scatter.25.cloned.1.call-done = bf16[128,1280]{1,0:T(8,128)(2,1)} async-done(((bf16[512,1280]{1,0:T(8,128)(2,1)}), bf16[128,1280]{1,0:T(8,128)(2,1)}) %reduce-scatter.25.cloned.1.call-update) | async-done | bytes 327696 | tf_op jit(solution)/shard_map/reduce_scatter | solution.py:224
  301.4 30.7 %all-gather.2 = bf16[8,1,640]{2,1,0:T(2,128)(2,1)S(1)} all-gather(bf16[1,1,640]{2,1,0:T(2,128)(2,1)S(1)} %reshape.1107), channel_id=1, replica_groups=mesh['dp'=8,'fsdp'=4] {'dp'}, dimensions={0}, use_global_device_ids=true | all-gather | bytes 11520 | tf_op jit(solution)/shard_map/all_gather | solution.py:169
  332.3 30.4 %all-gather.29.cloned.1.call-done = bf16[1280,1280]{1,0:T(8,128)(2,1)} async-done(((bf16[160,1280]{1,0:T(8,128)(2,1)}), bf16[1280,1280]{1,0:T(8,128)(2,1)}) %all-gather.29.cloned.1.call-update) | async-done | bytes 3276816 | tf_op jit(solution)/shard_map/all_gather | solution.py:161
  362.7 19.0 %all-gather.27.cloned.1.call-done = bf16[512,1280]{1,0:T(8,128)(2,1)} async-done(((bf16[128,1280]{1,0:T(8,128)(2,1)}), bf16[512,1280]{1,0:T(8,128)(2,1)}) %all-gather.27.cloned.1.call-update) | async-done | bytes 1310736 | tf_op jit(solution)/shard_map/all_gather | solution.py:235
  381.8 5.7 convolution_add_fusion.6
  387.5 58.5 %all-gather.31.cloned.1.call-done = bf16[1280,1280]{0,1:T(8,128)(2,1)} async-done(((bf16[1280,160]{0,1:T(8,128)(2,1)}), bf16[1280,1280]{0,1:T(8,128)(2,1)}) %all-gather.31.cloned.1.call-update) | async-done | bytes 3276816 | tf_op jit(solution)/shard_map/all_gather | solution.py:162
  446.0 6.0 convolution_convert_fusion.10
  452.7 39.3 %psum.71 = f32[]{:T(128)} all-reduce(f32[]{:T(128)} %convert_reduce_fusion.21), channel_id=1, replica_groups=mesh['dp'=8,'fsdp'=4] {'dp','fsdp'}, use_global_device_ids=true, to_apply=%region_29.30 | all-reduce | flops 1 | bytes 8 | tf_op jit(solution)/shard_map/psum | solution.py:143
  494.9 18.9 %all-gather.41.cloned.1.call-done = bf16[512,1280]{1,0:T(8,128)(2,1)} async-done(((bf16[128,1280]{1,0:T(8,128)(2,1)}), bf16[512,1280]{1,0:T(8,128)(2,1)}) %all-gather.41.cloned.1.call-update) | async-done | bytes 1310736 | tf_op jit(solution)/shard_map/all_gather | solution.py:253
  513.9 6.2 convert_reduce_fusion.2
  524.2 26.6 %reduce-scatter.29.cloned.1.call-done = bf16[128,1280]{1,0:T(8,128)(2,1)} async-done(((bf16[512,1280]{1,0:T(8,128)(2,1)}), bf16[128,1280]{1,0:T(8,128)(2,1)}) %reduce-scatter.29.cloned.1.call-update) | async-done | bytes 327696 | tf_op jit(solution)/shard_map/reduce_scatter | solution.py:266
  555.8 17.5 %all-gather.39.cloned.1.call-done = bf16[512,1280]{1,0:T(8,128)(2,1)} async-done(((bf16[128,1280]{1,0:T(8,128)(2,1)}), bf16[512,1280]{1,0:T(8,128)(2,1)}) %all-gather.39.cloned.1.call-update) | async-done | bytes 1310736 | tf_op jit(solution)/shard_map/all_gather | solution.py:235
  573.4 4.3 convolution_add_fusion.4
  579.3 3.3 convolution_convert_fusion.6
  582.6 11.1 all-gather.35.cloned.1.call-done
  593.7 4.3 convolution_add_fusion.5
  599.6 3.3 convolution_convert_fusion.8
  603.0 20.4 %reduce-scatter.27.cloned.1.call-done = bf16[128,1280]{1,0:T(8,128)(2,1)} async-done(((bf16[512,1280]{1,0:T(8,128)(2,1)}), bf16[128,1280]{1,0:T(8,128)(2,1)}) %reduce-scatter.27.cloned.1.call-update) | async-done | bytes 327696 | tf_op jit(solution)/shard_map/reduce_scatter | solution.py:238
  623.4 3.3 convert_reduce_fusion.20
  626.8 25.6 %reduce-scatter.23.cloned.1.call-done = bf16[128,1280]{1,0:T(8,128)(2,1)} async-done(((bf16[512,1280]{1,0:T(8,128)(2,1)}), bf16[128,1280]{1,0:T(8,128)(2,1)}) %reduce-scatter.23.cloned.1.call-update) | async-done | bytes 327696 | tf_op jit(solution)/shard_map/reduce_scatter | solution.py:238
  654.6 18.1 %all-gather.49.cloned.1.call-done = bf16[512,1280]{1,0:T(8,128)(2,1)} async-done(((bf16[128,1280]{1,0:T(8,128)(2,1)}), bf16[512,1280]{1,0:T(8,128)(2,1)}) %all-gather.49.cloned.1.call-update) | async-done | bytes 1310736 | tf_op jit(solution)/shard_map/all_gather | solution.py:253
  672.6 6.2 convert_reduce_fusion
  683.1 9.3 all-gather.45.cloned.1.call-done
  692.5 6.2 convert_reduce_fusion.1
  703.5 18.6 %reduce-scatter.37.cloned.1.call-done = bf16[128,1280]{1,0:T(8,128)(2,1)} async-done(((bf16[512,1280]{1,0:T(8,128)(2,1)}), bf16[128,1280]{1,0:T(8,128)(2,1)}) %reduce-scatter.37.cloned.1.call-update) | async-done | bytes 327696 | tf_op jit(solution)/shard_map/reduce_scatter | solution.py:266
  722.2 29.1 %reduce-scatter.33.cloned.1.call-done = bf16[128,1280]{1,0:T(8,128)(2,1)} async-done(((bf16[512,1280]{1,0:T(8,128)(2,1)}), bf16[128,1280]{1,0:T(8,128)(2,1)}) %reduce-scatter.33.cloned.1.call-update) | async-done | bytes 327696 | tf_op jit(solution)/shard_map/reduce_scatter | solution.py:266
  758.2 3.5 convert_reduce_fusion.18
  761.8 9.9 all-gather.43.cloned.1.call-done
  771.7 3.6 fusion.117
  775.3 16.3 %all-gather.47.cloned.1.call-done = bf16[512,1280]{1,0:T(8,128)(2,1)} async-done(((bf16[128,1280]{1,0:T(8,128)(2,1)}), bf16[512,1280]{1,0:T(8,128)(2,1)}) %all-gather.47.cloned.1.call-update) | async-done | bytes 1310736 | tf_op jit(solution)/shard_map/all_gather | solution.py:278
  791.6 4.2 convolution_add_fusion.8
  795.8 16.1 %all-gather.51.cloned.1.call-done = bf16[512,1280]{1,0:T(8,128)(2,1)} async-done(((bf16[128,1280]{1,0:T(8,128)(2,1)}), bf16[512,1280]{1,0:T(8,128)(2,1)}) %all-gather.51.cloned.1.call-update) | async-done | bytes 1310736 | tf_op jit(solution)/shard_map/all_gather | solution.py:278
  811.9 3.9 fusion.5
  815.9 3.8 fusion.197
  821.7 3.8 fusion
  908.4 4.0 fusion.180
  914.7 4.0 fusion.1
  925.8 3.7 fusion.12
  931.5 3.8 add_convert_fusion
  940.0 18.0 %reduce-scatter.45.cloned.1.call-done = bf16[160,1280]{1,0:T(8,128)(2,1)} async-done(((bf16[1280,1280]{1,0:T(8,128)(2,1)}), bf16[160,1280]{1,0:T(8,128)(2,1)}) %reduce-scatter.45.cloned.1.call-update) | async-done | bytes 409616 | tf_op jit(solution)/shard_map/reduce_scatter | solution.py:342
  959.9 26.2 %reduce-scatter.31.cloned.1.call-done = bf16[128,1280]{1,0:T(8,128)(2,1)} async-done(((bf16[512,1280]{1,0:T(8,128)(2,1)}), bf16[128,1280]{1,0:T(8,128)(2,1)}) %reduce-scatter.31.cloned.1.call-update) | async-done | bytes 327696 | tf_op jit(solution)/shard_map/reduce_scatter | solution.py:307
  986.1 29.7 %reduce-scatter.39.cloned.1.call-done = bf16[128,1280]{1,0:T(8,128)(2,1)} async-done(((bf16[512,1280]{1,0:T(8,128)(2,1)}), bf16[128,1280]{1,0:T(8,128)(2,1)}) %reduce-scatter.39.cloned.1.call-update) | async-done | bytes 327696 | tf_op jit(solution)/shard_map/reduce_scatter | solution.py:307
  1015.7 29.3 %reduce-scatter.35.cloned.1.call-done = bf16[128,1280]{1,0:T(8,128)(2,1)} async-done(((bf16[512,1280]{1,0:T(8,128)(2,1)}), bf16[128,1280]{1,0:T(8,128)(2,1)}) %reduce-scatter.35.cloned.1.call-update) | async-done | bytes 327696 | tf_op jit(solution)/shard_map/reduce_scatter | solution.py:307
  1047.2 77.4 %reduce-scatter.47.cloned.1.call-done = bf16[1280,160]{0,1:T(8,128)(2,1)} async-done(((bf16[1280,1280]{0,1:T(8,128)(2,1)}), bf16[1280,160]{0,1:T(8,128)(2,1)}) %reduce-scatter.47.cloned.1.call-update) | async-done | bytes 409616 | tf_op jit(solution)/shard_map/reduce_scatter | solution.py:345
  1126.5 43.1 %all-reduce.11 = (f32[]{:T(128)}, f32[1280]{0:T(1024)S(1)}, f32[1280]{0:T(1024)S(1)}, f32[3840]{0:T(1024)S(1)}, f32[1280]{0:T(1024)S(1)}, /*index=5*/f32[1280]{0...) all-reduce(f32[]{:T(128)S(6)} %add.553, ...), channel_id=1, replica_groups=mesh['dp'=8,'fsdp'=4] {'dp','fsdp'}, use_global_device_ids=true, to_apply=%region_27.28 | all-reduce | flops 16641 | bytes 133128 | tf_op jit(solution)/shard_map/psum | solution.py:349
  1180.4 20.7 %reduce-scatter.41.cloned.1.call-done = bf16[160,3,320]{2,0,1:T(8,128)(2,1)} async-done(((bf16[1280,3,320]{2,0,1:T(8,128)(2,1)}), bf16[160,3,320]{2,0,1:T(8,128)(2,1)}) %reduce-scatter.41.cloned.1.call-update) | async-done | bytes 307216 | tf_op jit(solution)/shard_map/reduce_scatter | solution.py:336
  (621 shorter events, 238.0 us)
Async XLA Ops:
  7.2 55.4 %copy-start.129 = (s32[384,2]{0,1:T(2,128)S(1)}, s32[384,2]{0,1:T(2,128)}, u32[]{:S(2)}) copy-start(s32[384,2]{0,1:T(2,128)} %param.20) | copy-start | bytes 9220
  7.2 55.4 %copy-start.105 = (s32[384]{0:T(512)S(1)}, s32[384]{0:T(512)}, u32[]{:S(2)}) copy-start(s32[384]{0:T(512)} %param.21) | copy-start | bytes 4612
  7.2 61.0 %copy-start.117 = (s32[384]{0:T(512)S(1)}, s32[384]{0:T(512)}, u32[]{:S(2)}) copy-start(s32[384]{0:T(512)} %param.19) | copy-start | bytes 4612
  7.2 107.9 %copy-start.76 = (bf16[320,160]{0,1:T(8,128)(2,1)S(1)}, bf16[320,160]{0,1:T(8,128)(2,1)}, u32[]{:S(2)}) copy-start(bf16[320,160]{0,1:T(8,128)(2,1)} %param.26) | copy-start | bytes 307204
  7.2 140.6 %all-gather.25.cloned.1.call-start = ((), (), s32[]{:S(2)}) async-start(), calls=%async_computation.17 | async-start | bytes 3317760 | tf_op jit(solution)/shard_map/all_gather | solution.py:159
  8.0 145.6 %all-gather.23.cloned.1.call-start = ((), (), s32[]{:S(2)}) async-start(), calls=%async_computation.16 | async-start | bytes 1638400 | tf_op jit(solution)/shard_map/all_gather | solution.py:201
  57.2 54.0 %copy-start.77 = (f32[1280]{0:T(1024)}, f32[1280]{0:T(1024)S(1)}, u32[]{:S(2)}) copy-start(f32[1280]{0:T(1024)S(1)} %convert_element_type.441) | copy-start | bytes 15364
  57.2 139.8 %copy-start.71 = (f32[1280]{0:T(1024)}, f32[1280]{0:T(1024)S(1)}, u32[]{:S(2)}) copy-start(f32[1280]{0:T(1024)S(1)} %convert_element_type.440) | copy-start | bytes 15364
  62.3 132.9 %reduce-scatter.17.cloned.1.call-start = ((), (), s32[]{:S(2)}) async-start(), calls=%async_computation.18 | async-start | bytes 1638400 | tf_op jit(solution)/shard_map/reduce_scatter | solution.py:224
  62.5 91.0 %copy-start.126 = (f32[960]{0:T(1024)}, f32[960]{0:T(1024)S(1)}, u32[]{:S(2)}) copy-start(f32[960]{0:T(1024)S(1)} %reshape.1081) | copy-start | bytes 11524
  111.0 42.5 %copy-start.130 = (f32[20]{0:T(128)}, f32[20]{0:T(128)S(1)}, u32[]{:S(2)}) copy-start(f32[20]{0:T(128)S(1)} %negate_power_fusion) | copy-start | bytes 244
  111.1 42.4 %copy-start.82 = (f32[512,1]{0,1:T(1,128)}, f32[512,1]{0,1:T(1,128)S(1)}, u32[]{:S(2)}) copy-start(f32[512,1]{0,1:T(1,128)S(1)} %get-tuple-element.182) | copy-start | bytes 6148
  111.1 42.4 %copy-start.84 = (f32[512,1]{0,1:T(1,128)}, f32[512,1]{0,1:T(1,128)S(1)}, u32[]{:S(2)}) copy-start(f32[512,1]{0,1:T(1,128)S(1)} %get-tuple-element.183) | copy-start | bytes 6148
  171.1 45.5 %copy-start.127 = (f32[960]{0:T(1024)S(1)}, f32[960]{0:T(1024)}, u32[]{:S(2)}) copy-start(f32[960]{0:T(1024)} %copy-done.126) | copy-start | bytes 11524
  171.1 45.4 %all-gather.33.cloned.1.call-start = ((), (), s32[]{:S(2)}) async-start(), calls=%async_computation.23 | async-start | bytes 1638400 | tf_op jit(solution)/shard_map/all_gather | solution.py:201
  171.3 48.9 %copy-start.92 = (f32[128]{0:T(128)}, f32[128]{0:T(128)S(1)}, u32[]{:S(2)}) copy-start(f32[128]{0:T(128)S(1)} %get-tuple-element.231) | copy-start | bytes 1540
  171.3 48.9 %copy-start.94 = (f32[128]{0:T(128)}, f32[128]{0:T(128)S(1)}, u32[]{:S(2)}) copy-start(f32[128]{0:T(128)S(1)} %get-tuple-element.230) | copy-start | bytes 1540
  198.2 42.2 %all-gather.37.cloned.1.call-start = ((), (), s32[]{:S(2)}) async-start(), calls=%async_computation.27 | async-start | bytes 1638400 | tf_op jit(solution)/shard_map/all_gather | solution.py:201
  201.9 70.6 %reduce-scatter.21.cloned.1.call-start = ((), (), s32[]{:S(2)}) async-start(), calls=%async_computation.24 | async-start | bytes 1638400 | tf_op jit(solution)/shard_map/reduce_scatter | solution.py:224
  240.4 57.9 %reduce-scatter.25.cloned.1.call-start = ((), (), s32[]{:S(2)}) async-start(), calls=%async_computation.28 | async-start | bytes 1638400 | tf_op jit(solution)/shard_map/reduce_scatter | solution.py:224
  271.6 91.1 %all-gather.29.cloned.1.call-start = ((), (), s32[]{:S(2)}) async-start(), calls=%async_computation.20 | async-start | bytes 3686400 | tf_op jit(solution)/shard_map/all_gather | solution.py:161
  272.3 109.4 %all-gather.27.cloned.1.call-start = ((), (), s32[]{:S(2)}) async-start(), calls=%async_computation.19 | async-start | bytes 1638400 | tf_op jit(solution)/shard_map/all_gather | solution.py:235
  300.7 145.3 %all-gather.31.cloned.1.call-start = ((), (), s32[]{:S(2)}) async-start(), calls=%async_computation.21 | async-start | bytes 3686400 | tf_op jit(solution)/shard_map/all_gather | solution.py:162
  301.3 191.5 %reduce-scatter.19.cloned.1.call-start = ((), (), s32[]{:S(2)}) async-start(), calls=%async_computation.22 | async-start | bytes 1638400 | tf_op jit(solution)/shard_map/reduce_scatter | solution.py:238
  387.5 64.6 %copy-start.106 = (s32[384]{0:T(512)S(1)}, s32[384]{0:T(512)}, u32[]{:S(2)}) copy-start(s32[384]{0:T(512)} %param.21) | copy-start | bytes 4612
  387.5 104.5 %copy-start.122 = (bf16[1280]{0:T(1024)(128)(2,1)S(1)}, bf16[1280]{0:T(1024)(128)(2,1)}, u32[]{:S(2)}) copy-start(bf16[1280]{0:T(1024)(128)(2,1)} %get-tuple-element.69) | copy-start | bytes 7684
  387.5 105.2 %copy-start.112 = (f32[384]{0:T(512)S(1)}, f32[384]{0:T(512)}, u32[]{:S(2)}) copy-start(f32[384]{0:T(512)} %get-tuple-element.180) | copy-start | bytes 4612
  452.0 61.8 %all-gather.41.cloned.1.call-start = ((), (), s32[]{:S(2)}) async-start(), calls=%async_computation.31 | async-start | bytes 1638400 | tf_op jit(solution)/shard_map/all_gather | solution.py:253
  492.7 130.7 %copy-start.98 = (f32[128]{0:T(128)}, f32[128]{0:T(128)S(1)}, u32[]{:S(2)}) copy-start(f32[128]{0:T(128)S(1)} %get-tuple-element.178) | copy-start | bytes 1540
  492.7 130.7 %copy-start.101 = (f32[128]{0:T(128)}, f32[128]{0:T(128)S(1)}, u32[]{:S(2)}) copy-start(f32[128]{0:T(128)S(1)} %get-tuple-element.179) | copy-start | bytes 1540
  492.7 261.2 %copy-start.96 = (f32[128]{0:T(128)}, f32[128]{0:T(128)S(1)}, u32[]{:S(2)}) copy-start(f32[128]{0:T(128)S(1)} %get-tuple-element.177) | copy-start | bytes 1540
  494.9 55.9 %reduce-scatter.29.cloned.1.call-start = ((), (), s32[]{:S(2)}) async-start(), calls=%async_computation.32 | async-start | bytes 1638400 | tf_op jit(solution)/shard_map/reduce_scatter | solution.py:266
  524.1 49.3 %all-gather.39.cloned.1.call-start = ((), (), s32[]{:S(2)}) async-start(), calls=%async_computation.29 | async-start | bytes 1638400 | tf_op jit(solution)/shard_map/all_gather | solution.py:235
  524.2 227.1 %copy-start.111 = (f32[128]{0:T(128)}, f32[128]{0:T(128)S(1)}, u32[]{:S(2)}) copy-start(f32[128]{0:T(128)S(1)} %broadcast_multiply_fusion.26) | copy-start | bytes 1540
  524.2 227.1 %copy-start.110 = (f32[128]{0:T(128)}, f32[128]{0:T(128)S(1)}, u32[]{:S(2)}) copy-start(f32[128]{0:T(128)S(1)} %broadcast_multiply_fusion.24) | copy-start | bytes 1540
  555.0 38.6 %all-gather.35.cloned.1.call-start = ((), (), s32[]{:S(2)}) async-start(), calls=%async_computation.25 | async-start | bytes 1638400 | tf_op jit(solution)/shard_map/all_gather | solution.py:235
  555.6 67.7 %reduce-scatter.27.cloned.1.call-start = ((), (), s32[]{:S(2)}) async-start(), calls=%async_computation.30 | async-start | bytes 1638400 | tf_op jit(solution)/shard_map/reduce_scatter | solution.py:238
  582.5 69.8 %reduce-scatter.23.cloned.1.call-start = ((), (), s32[]{:S(2)}) async-start(), calls=%async_computation.26 | async-start | bytes 1638400 | tf_op jit(solution)/shard_map/reduce_scatter | solution.py:238
  602.9 69.7 %all-gather.49.cloned.1.call-start = ((), (), s32[]{:S(2)}) async-start(), calls=%async_computation.39 | async-start | bytes 1638400 | tf_op jit(solution)/shard_map/all_gather | solution.py:253
  626.7 65.8 %all-gather.45.cloned.1.call-start = ((), (), s32[]{:S(2)}) async-start(), calls=%async_computation.35 | async-start | bytes 1638400 | tf_op jit(solution)/shard_map/all_gather | solution.py:253
  654.5 67.7 %reduce-scatter.37.cloned.1.call-start = ((), (), s32[]{:S(2)}) async-start(), calls=%async_computation.40 | async-start | bytes 1638400 | tf_op jit(solution)/shard_map/reduce_scatter | solution.py:266
  682.9 68.4 %reduce-scatter.33.cloned.1.call-start = ((), (), s32[]{:S(2)}) async-start(), calls=%async_computation.36 | async-start | bytes 1638400 | tf_op jit(solution)/shard_map/reduce_scatter | solution.py:266
  702.7 69.0 %all-gather.43.cloned.1.call-start = ((), (), s32[]{:S(2)}) async-start(), calls=%async_computation.33 | async-start | bytes 1638400 | tf_op jit(solution)/shard_map/all_gather | solution.py:278
  703.5 54.8 %copy-start.99 = (f32[128]{0:T(128)S(1)}, f32[128]{0:T(128)}, u32[]{:S(2)}) copy-start(f32[128]{0:T(128)} %copy-done.98) | copy-start | bytes 1540
  703.5 88.1 %all-gather.47.cloned.1.call-start = ((), (), s32[]{:S(2)}) async-start(), calls=%async_computation.37 | async-start | bytes 1638400 | tf_op jit(solution)/shard_map/all_gather | solution.py:278
  756.9 55.0 %all-gather.51.cloned.1.call-start = ((), (), s32[]{:S(2)}) async-start(), calls=%async_computation.41 | async-start | bytes 1638400 | tf_op jit(solution)/shard_map/all_gather | solution.py:278
  761.8 176.6 %reduce-scatter.43.cloned.1.call-start = ((), (), s32[]{:S(2)}) async-start(), calls=%async_computation.44 | async-start | bytes 1105920 | tf_op jit(solution)/shard_map/reduce_scatter | solution.py:339
  815.8 142.1 %reduce-scatter.45.cloned.1.call-start = ((), (), s32[]{:S(2)}) async-start(), calls=%async_computation.45 | async-start | bytes 3686400 | tf_op jit(solution)/shard_map/reduce_scatter | solution.py:342
  825.6 160.5 %reduce-scatter.31.cloned.1.call-start = ((), (), s32[]{:S(2)}) async-start(), calls=%async_computation.34 | async-start | bytes 1638400 | tf_op jit(solution)/shard_map/reduce_scatter | solution.py:307
  858.0 157.7 %reduce-scatter.39.cloned.1.call-start = ((), (), s32[]{:S(2)}) async-start(), calls=%async_computation.42 | async-start | bytes 1638400 | tf_op jit(solution)/shard_map/reduce_scatter | solution.py:307
  895.6 149.5 %reduce-scatter.35.cloned.1.call-start = ((), (), s32[]{:S(2)}) async-start(), calls=%async_computation.38 | async-start | bytes 1638400 | tf_op jit(solution)/shard_map/reduce_scatter | solution.py:307
  908.3 216.2 %reduce-scatter.47.cloned.1.call-start = ((), (), s32[]{:S(2)}) async-start(), calls=%async_computation.46 | async-start | bytes 3686400 | tf_op jit(solution)/shard_map/reduce_scatter | solution.py:345
  918.8 282.3 %reduce-scatter.41.cloned.1.call-start = ((), (), s32[]{:S(2)}) async-start(), calls=%async_computation.43 | async-start | bytes 3317760 | tf_op jit(solution)/shard_map/reduce_scatter | solution.py:336
  935.3 109.7 %copy-start.72 = (f32[1280]{0:T(1024)S(1)}, f32[1280]{0:T(1024)}, u32[]{:S(2)}) copy-start(f32[1280]{0:T(1024)} %copy-done.71) | copy-start | bytes 15364
  935.3 109.7 %copy-start.93 = (f32[128]{0:T(128)S(1)}, f32[128]{0:T(128)}, u32[]{:S(2)}) copy-start(f32[128]{0:T(128)} %copy-done.92) | copy-start | bytes 1540
  935.3 109.7 %copy-start.95 = (f32[128]{0:T(128)S(1)}, f32[128]{0:T(128)}, u32[]{:S(2)}) copy-start(f32[128]{0:T(128)} %copy-done.94) | copy-start | bytes 1540
  935.3 109.7 %copy-start.109 = (f32[128]{0:T(128)S(1)}, f32[128]{0:T(128)}, u32[]{:S(2)}) copy-start(f32[128]{0:T(128)} %copy-done.108) | copy-start | bytes 1540
  935.4 109.7 %copy-start.114 = (f32[128]{0:T(128)S(1)}, f32[128]{0:T(128)}, u32[]{:S(2)}) copy-start(f32[128]{0:T(128)} %copy-done.113) | copy-start | bytes 1540
  935.4 109.7 %copy-start.116 = (f32[128]{0:T(128)S(1)}, f32[128]{0:T(128)}, u32[]{:S(2)}) copy-start(f32[128]{0:T(128)} %copy-done.115) | copy-start | bytes 1540
  935.4 109.7 %copy-start.119 = (f32[128]{0:T(128)S(1)}, f32[128]{0:T(128)}, u32[]{:S(2)}) copy-start(f32[128]{0:T(128)} %copy-done.118) | copy-start | bytes 1540
  937.7 238.5 %copy-start.31 = (f32[128,1280]{1,0:T(8,128)S(1)}, f32[128,1280]{1,0:T(8,128)}, u32[]{:S(2)}) copy-start(f32[128,1280]{1,0:T(8,128)} %get-tuple-element.90) | copy-start | bytes 1966084
  959.9 217.5 %copy-start.30 = (f32[128,1280]{1,0:T(8,128)S(1)}, f32[128,1280]{1,0:T(8,128)}, u32[]{:S(2)}) copy-start(f32[128,1280]{1,0:T(8,128)} %get-tuple-element.87) | copy-start | bytes 1966084
  959.9 217.6 %copy-start.38 = (f32[128,1280]{1,0:T(8,128)S(1)}, f32[128,1280]{1,0:T(8,128)}, u32[]{:S(2)}) copy-start(f32[128,1280]{1,0:T(8,128)} %get-tuple-element.84) | copy-start | bytes 1966084
  986.1 191.4 %copy-start.45 = (bf16[128,1280]{1,0:T(8,128)(2,1)S(1)}, bf16[128,1280]{1,0:T(8,128)(2,1)}, u32[]{:S(2)}) copy-start(bf16[128,1280]{1,0:T(8,128)(2,1)} %reduce-scatter.31.cloned.1.call-done) | copy-start | bytes 983044
  (119 other events, 791.1 us)
Sparse Core Ops, SparseCore 0:
  10.2 61.7 all-gather.24
  74.2 16.9 all-gather.22
  171.3 23.8 reduce-scatter.16
  198.4 18.1 all-gather.32
  218.7 18.1 all-gather.36
  240.5 26.5 reduce-scatter.20
  271.7 26.4 reduce-scatter.24
  300.6 62.0 all-gather.28
  364.9 16.7 all-gather.26
  384.0 61.9 all-gather.30
  452.1 25.1 reduce-scatter.18
  495.0 18.8 all-gather.40
  524.2 26.5 reduce-scatter.28
  555.2 18.1 all-gather.38
  575.4 18.1 all-gather.34
  596.8 26.5 reduce-scatter.26
  625.8 26.5 reduce-scatter.22
  654.4 18.1 all-gather.48
  674.2 18.1 all-gather.44
  695.6 26.5 reduce-scatter.36
  724.7 26.5 reduce-scatter.32
  753.5 18.1 all-gather.42
  773.4 18.1 all-gather.46
  793.7 18.1 all-gather.50
  816.0 63.2 reduce-scatter.42
  882.7 75.1 reduce-scatter.44
  960.5 25.5 reduce-scatter.30
  989.2 26.5 reduce-scatter.38
  1018.4 26.5 reduce-scatter.34
  1048.5 76.0 reduce-scatter.46
  1128.6 72.4 reduce-scatter.40
where the time goes:
time: 1220 us; the launch traced here: 1210 us
  waiting for transfers between devices  614 us (50%)
  blocking collectives  232 us (19%)
  matrix products  145 us (12%)
  local copies, waits for them, and re-layouts  106 us (9%)
  other arithmetic  87.7 us (7%)
  between operations  24 us (2%)
    reduce_scatter x3, waiting for transfers between devices, on_device(): lax.psum_scatter(jnp.einsum('re,de->rd', grad_mixed, mixer_flat, preferre...  85.1 us
    reduce_scatter x1, waiting for transfers between devices, on_device(): lax.psum_scatter(g_down_sum.astype(jnp.bfloat16), 'dp', scatter_dimension...  77.4 us
    reduce_scatter x3, waiting for transfers between devices, on_device(): lax.psum_scatter(jnp.einsum('rf,df->rd', grad_upper, upward_local, prefer...  74.3 us
    all_gather x1, waiting for transfers between devices, on_device(): lax.all_gather(downward_weight, 'dp', axis=1, tiled=True)  58.5 us
    reduce_scatter x3, waiting for transfers between devices, on_device(): lax.psum_scatter(jnp.dot(attended, output_local, preferred_element_type=j...  49.7 us
    all_gather x3, waiting for transfers between devices, on_device(): group_two = lax.all_gather(lowered_two, 'fsdp', axis=0, tiled=True)  47.6 us
    all_gather x3, waiting for transfers between devices, on_device(): group_grad = lax.all_gather(grad_low, 'fsdp', axis=0, tiled=True)  46.4 us
    reduce_scatter x3, waiting for transfers between devices, on_device(): lax.psum_scatter(jnp.dot(active, downward_local, preferred_element_type=j...  46 us
  transfers between devices with their start and end apart: 31, of which 25 were waited for; matrix products, arithmetic and copies ran while one was open for 22% of the time, Pallas kernels for 0%

commit v1 on v0

--- a/solution.py
+++ b/solution.py
@@ -1,6 +1,9 @@
+import numpy as np
 import jax
 import jax.numpy as jnp
 from jax import lax
+from jax.experimental import pallas as pl
+from jax.experimental.pallas import tpu as pltpu
 from jax.sharding import PartitionSpec as P
 
 D = 1280
@@ -384,9 +387,1027 @@
     )
 
 
+BF = jnp.bfloat16
+F32 = jnp.float32
+HEADS_LOCAL = 4
+W = 320
+F = 1280
+R = 384
+G = 1536
+BLK = 160
+MESH_ID = pl.DeviceIdType.MESH
+
+
+def _nn(a, b):
+    return lax.dot_general(a, b, (((1,), (0,)), ((), ())), preferred_element_type=F32)
+
+
+def _nt(a, b):
+    return lax.dot_general(a, b, (((1,), (1,)), ((), ())), preferred_element_type=F32)
+
+
+def _tn(a, b):
+    return lax.dot_general(a, b, (((0,), (0,)), ((), ())), preferred_element_type=F32)
+
+
+def _rows(start, size, step):
+    return pl.ds(pl.multiple_of(start, step), size)
+
+
+class Place:
+    def __init__(self):
+        dp = lax.axis_index("dp")
+        fs = lax.axis_index("fsdp")
+        z, x = lax.div(dp, 2), lax.rem(dp, 2)
+        y, c = lax.div(fs, 2), lax.rem(fs, 2)
+        self.z, self.x, self.fs = z, x, fs
+        self.core = (dp, 2 * y + 1 - c)
+        self.ynb = (dp, 2 * (1 - y) + c)
+        self.xnb = (2 * z + 1 - x, fs)
+        self.zs = (z, z + 1 - 2 * lax.rem(z, 2), lax.rem(z + 2, 4), 3 - z)
+        self.zn = tuple((2 * zk + x, fs) for zk in self.zs)
+
+    def barrier(self):
+        sem = pltpu.get_barrier_semaphore()
+        for peer in (self.core, self.ynb, self.xnb) + self.zn[1:]:
+            pl.semaphore_signal(sem, inc=1, device_id=peer, device_id_type=MESH_ID)
+        pl.semaphore_wait(sem, 6)
+
+
+def _send(src, dst, ss, rs, peer):
+    return pltpu.make_async_remote_copy(
+        src_ref=src, dst_ref=dst, send_sem=ss, recv_sem=rs, device_id=peer, device_id_type=MESH_ID
+    )
+
+
+class Gather:
+    def __init__(self, place, buf, ss, rs):
+        self.to_core = _send(
+            buf.at[pl.ds(0, R), :], buf.at[pl.ds(R, R), :], ss.at[0], rs.at[0], place.core
+        )
+        self.to_y = [
+            _send(
+                buf.at[pl.ds(128 * i, 128), :],
+                buf.at[pl.ds(2 * R + 128 * i, 128), :],
+                ss.at[1 + i],
+                rs.at[1 + i],
+                place.ynb,
+            )
+            for i in range(3)
+        ]
+        self.on = [
+            _send(
+                buf.at[pl.ds(2 * R + 128 * i, 128), :],
+                buf.at[pl.ds(3 * R + 128 * i, 128), :],
+                ss.at[4 + i],
+                rs.at[4 + i],
+                place.core,
+            )
+            for i in range(3)
+        ]
+
+    def start_y(self, i):
+        self.to_y[i].start()
+
+    def start_core(self):
+        self.to_core.start()
+
+    def start(self):
+        for copy in self.to_y:
+            copy.start()
+        self.to_core.start()
+
+    def wait_core(self):
+        self.to_core.wait_recv()
+
+    def pass_on(self):
+        for here, on in zip(self.to_y, self.on):
+            here.wait_recv()
+            on.start()
+
+    def wait_diagonal(self):
+        for on in self.on:
+            on.wait_recv()
+
+    def end(self):
+        self.to_core.wait_send()
+        for copy in self.to_y + self.on:
+            copy.wait_send()
+
+
+class Scatter:
+    def __init__(self, place, sb, rb, ss, rs):
+        self.sb, self.rb = sb, rb
+        peers = (place.core, place.ynb, place.core)
+        self.copies = [_send(sb.at[i], rb.at[i], ss.at[i], rs.at[i], peers[i]) for i in range(3)]
+
+    def diagonal(self, term):
+        self.sb[0] = term.astype(BF)
+        self.copies[0].start()
+
+    def over_y(self, term):
+        self.copies[0].wait_recv()
+        self.sb[1] = (term + self.rb[0].astype(F32)).astype(BF)
+        self.copies[1].start()
+
+    def other_core(self, term):
+        self.sb[2] = term.astype(BF)
+        self.copies[2].start()
+
+    def wait(self):
+        self.copies[2].wait_recv()
+        self.copies[1].wait_recv()
+
+    def rest(self, rows):
+        return self.rb[2, rows, :].astype(F32) + self.rb[1, rows, :].astype(F32)
+
+    def end(self):
+        for copy in self.copies:
+            copy.wait_send()
+
+
+def _norm(values):
+    average = jnp.mean(values, axis=-1, keepdims=True)
+    centered = values - average
+    reciprocal = lax.rsqrt(jnp.mean(centered * centered, axis=-1, keepdims=True) + EPSILON)
+    return centered * reciprocal, reciprocal
+
+
+def _head_rows(lanes, offset):
+    lane = lax.broadcasted_iota(jnp.int32, (1, lanes), 1) - offset
+    return [
+        jnp.where((lane >= HD * h) & (lane < HD * h + HD), 1.0, 0.0).astype(BF)
+        for h in range(HEADS_LOCAL)
+    ]
+
+
+def _stack(values, heads):
+    return jnp.concatenate([values * head for head in heads], axis=0)
+
+
+def _allowed(auxb):
+    lane = lax.broadcasted_iota(jnp.int32, (1, 128), 1)
+    picks = (lane >= 96) & (lane < 104)
+    left = jnp.where(picks, auxb.astype(F32), jnp.where(lane == 104, 1.0, 0.0)).astype(BF)
+    score = _nt(left, auxb)
+    here = lax.broadcasted_iota(jnp.int32, (128, 128), 0)
+    there = lax.broadcasted_iota(jnp.int32, (128, 128), 1)
+    return (score > 1.5) | (here == there)
+
+
+def _softmax(scores, allowed):
+    probs = []
+    for h in range(HEADS_LOCAL):
+        part = jnp.where(allowed, scores[:, 128 * h : 128 * h + 128], -1e30)
+        grown = jnp.exp(part - jnp.max(part, axis=-1, keepdims=True))
+        probs.append(grown * (1.0 / jnp.sum(grown, axis=-1, keepdims=True)))
+    return probs
+
+
+def forward_kernel(
+    tok_h, teach_h, aux_h, wa_h, wu_h, wd_h, vecs, mixb, tabs,
+    res_h, gz_h, gy_h, mid_h, n1_h, n2_h, act_h, da_h, qk_h, v_h, o_h, aux_o, w_h, err_o,
+    tok, teach, aux, w, wo, n1, n2, act, da, qk, v, o, mix, acc, mid, gy, sb, rb,
+    ws, wr, ns, nr, xs, xr, ts, tr, ps, pr, ls, os_,
+):
+    place = Place()
+    local = [
+        pltpu.make_async_copy(src, dst, ls.at[i])
+        for i, (src, dst) in enumerate(
+            [
+                (tok_h, tok),
+                (aux_h, aux.at[pl.ds(0, R), :]),
+                (teach_h, teach),
+                (wa_h, w.at[0, _rows(BLK * (2 * place.z + place.x), BLK, 32), :]),
+                (wu_h, w.at[1, _rows(BLK * (2 * place.z + place.x), BLK, 32), :]),
+                (wd_h, w.at[2, _rows(BLK * (2 * place.z + place.x), BLK, 32), :]),
+            ]
+        )
+    ]
+    for copy in local:
+        copy.start()
+    place.barrier()
+
+    shards = (wa_h, wu_h, wd_h)
+
+    def at(chunk, zk, xk):
+        return w.at[chunk, _rows(BLK * (2 * zk + xk), BLK, 32), :]
+
+    def block(chunk, zk, xk):
+        return wr.at[chunk, 2 * zk + xk]
+
+    def first(chunk, k):
+        z, x = place.z, place.x
+        peer = place.xnb if k == 0 else place.zn[k]
+        return _send(shards[chunk], at(chunk, z, x), ws.at[chunk, k], block(chunk, z, x), peer)
+
+    def second(chunk, k):
+        zk, x = place.zs[k], place.x
+        return _send(
+            at(chunk, zk, x), at(chunk, zk, x), ws.at[chunk, 3 + k], block(chunk, zk, x), place.xnb
+        )
+
+    def begin(chunk):
+        for k in range(4):
+            first(chunk, k).start()
+
+    def onward(chunk, k):
+        second(chunk, k).wait_recv()
+        second(chunk, k).start()
+
+    def complete(chunk):
+        for zk in range(4):
+            _send(
+                at(chunk, zk, 1 - place.x),
+                at(chunk, zk, 1 - place.x),
+                ws.at[chunk, 0],
+                block(chunk, zk, 1 - place.x),
+                place.xnb,
+            ).wait_recv()
+        local[3 + chunk].wait()
+
+    outs = []
+
+    def out(src, dst):
+        copy = pltpu.make_async_copy(src, dst, os_.at[len(outs)])
+        copy.start()
+        outs.append(copy)
+
+    begin(0)
+    local[0].wait()
+    ag1 = Gather(place, n1, ns, nr)
+    agx = Gather(place, aux, xs, xr)
+    local[1].wait()
+    agx.start()
+
+    def first_norm(i, _):
+        rows = _rows(32 * i, 32, 32)
+        normed, _r = _norm(tok[rows, :].astype(F32))
+        n1[rows, :] = (normed * vecs[0:1, :] + vecs[1:2, :]).astype(BF)
+        return 0
+
+    lax.fori_loop(0, R // 32, first_norm, 0)
+    ag1.start()
+    agx.pass_on()
+    onward(0, 1)
+    ag1.pass_on()
+    onward(0, 3)
+    onward(0, 2)
+    begin(1)
+    ag1.wait_core()
+    ag1.wait_diagonal()
+    agx.wait_core()
+    agx.wait_diagonal()
+    complete(0)
+    wo[...] = w[0, :, 3 * W :]
+    out(n1, n1_h)
+    out(aux, aux_o)
+    out(w.at[0], w_h.at[0])
+
+    left = _head_rows(2 * W, 0)
+    side = _head_rows(W, 0)
+    rs1 = Scatter(place, sb, rb, ts, tr)
+
+    def member(t, _):
+        r = 3 - t
+        mix[...] = (
+            _nn(n1[_rows(R * r, R, 128), :], w[0, :, : 3 * W]) + mixb[...]
+        )
+
+        def attend_rows(i, _):
+            mine = _rows(128 * i, 128, 128)
+            rows = _rows(R * r + 128 * i, 128, 128)
+            auxb = aux[rows, :]
+            angle = _nn(auxb, tabs[...])
+            raw = mix[mine, : 2 * W]
+            turned = (
+                raw * angle[:, : 2 * W]
+                + pltpu.roll(raw, 2 * W - 40, 1) * angle[:, 2 * W : 4 * W]
+                + pltpu.roll(raw, 40, 1) * angle[:, 4 * W :]
+            )
+            qkb = turned.astype(BF)
+            kqb = pltpu.roll(turned, W, 1).astype(BF)
+            vb = mix[mine, 2 * W :].astype(BF)
+            qk[rows, :] = qkb
+            v[rows, :] = vb
+            scores = _nt(qkb, _stack(kqb, left)) * HD ** (-0.5)
+            probs = _softmax(scores, _allowed(auxb))
+            flat = jnp.concatenate([p.astype(BF) for p in probs], axis=1)
+            o[rows, :] = _nn(flat, _stack(vb, side)).astype(BF)
+            return 0
+
+        lax.fori_loop(0, 3, attend_rows, 0)
+        acc[...] = _nt(o[_rows(R * r, R, 128), :], wo[...])
+
+        @pl.when(t == 0)
+        def _():
+            rs1.diagonal(acc[...])
+            onward(1, 1)
+
+        @pl.when(t == 1)
+        def _():
+            rs1.over_y(acc[...])
+            onward(1, 3)
+
+        @pl.when(t == 2)
+        def _():
+            rs1.other_core(acc[...])
+            onward(1, 2)
+
+        return 0
+
+    lax.fori_loop(0, 4, member, 0)
+    begin(2)
+    out(qk, qk_h)
+    out(v, v_h)
+    out(o, o_h)
+    rs1.wait()
+
+    ns2 = Gather(place, n2, ns, nr)
+    ag1.end()
+
+    def second_norm(i, _):
+        rows = _rows(32 * i, 32, 32)
+        middle = tok[rows, :].astype(F32) + (acc[rows, :] + rs1.rest(rows)) + vecs[2:3, :]
+        mid[rows, :] = middle
+        normed, _r = _norm(middle)
+        n2[rows, :] = (normed * vecs[3:4, :] + vecs[4:5, :]).astype(BF)
+        return 0
+
+    lax.fori_loop(0, R // 32, second_norm, 0)
+    ns2.start()
+    out(mid, mid_h)
+    complete(1)
+    out(w.at[1], w_h.at[1])
+
+    def upward(r):
+        rows = _rows(R * r, R, 128)
+        acc[...] = _nn(n2[rows, :], w[1]) + vecs[6:7, :]
+
+        def active_rows(i, _):
+            sub = _rows(32 * i, 32, 32)
+            rows = _rows(R * r + 32 * i, 32, 32)
+            upper = acc[sub, :]
+            gate = 1.0 / (1.0 + jnp.exp(-1.702 * upper))
+            act[rows, :] = (upper * gate).astype(BF)
+            da[rows, :] = (gate + 1.702 * upper * gate * (1.0 - gate)).astype(BF)
+            return 0
+
+        lax.fori_loop(0, R // 32, active_rows, 0)
+
+    def up_members(r, _):
+        @pl.when(r == 1)
+        def _():
+            ns2.wait_core()
+
+        @pl.when(r == 2)
+        def _():
+            onward(2, 1)
+            ns2.pass_on()
+
+        @pl.when(r == 3)
+        def _():
+            onward(2, 3)
+            ns2.wait_diagonal()
+
+        upward(r)
+        return 0
+
+    lax.fori_loop(0, 4, up_members, 0)
+    out(n2, n2_h)
+    out(act, act_h)
+    out(da, da_h)
+    onward(2, 2)
+    complete(2)
+    out(w.at[2], w_h.at[2])
+    rs1.end()
+    rs2 = Scatter(place, sb, rb, ps, pr)
+
+    def down_members(t, _):
+        acc[...] = _nt(act[_rows(R * (3 - t), R, 128), :], w[2])
+
+        @pl.when(t == 0)
+        def _():
+            rs2.diagonal(acc[...])
+
+        @pl.when(t == 1)
+        def _():
+            rs2.over_y(acc[...])
+
+        @pl.when(t == 2)
+        def _():
+            rs2.other_core(acc[...])
+
+        return 0
+
+    lax.fori_loop(0, 4, down_members, 0)
+    local[2].wait()
+    rs2.wait()
+    agx.end()
+
+    def finish(i, total):
+        rows = _rows(32 * i, 32, 32)
+        result = mid[rows, :] + (acc[rows, :] + rs2.rest(rows)) + vecs[5:6, :]
+        real = aux[rows, 104:105].astype(F32)
+        difference = result - teach[rows, :].astype(F32)
+        masked = real * difference
+        gout = vecs[7:8, :] * masked
+        gy[rows, :] = gout
+        tok[rows, :] = result.astype(BF)
+        teach[rows, :] = gout.astype(BF)
+        return total + jnp.sum(masked * difference, axis=0, keepdims=True)
+
+    total = lax.fori_loop(0, R // 32, finish, jnp.zeros((1, D), F32))
+    err_o[...] = jnp.broadcast_to(total, (8, D))
+    out(tok, res_h)
+    out(teach, gz_h)
+    out(gy, gy_h)
+    ns2.end()
+    rs2.end()
+    for chunk in range(3):
+        for k in range(4):
+            first(chunk, k).wait_send()
+        for k in range(1, 4):
+            second(chunk, k).wait_send()
+    for copy in outs:
+        copy.wait()
+
+
+def _call(kernel, name, outs, ins, scratch, collective, limit):
+    return pl.pallas_call(
+        kernel,
+        out_shape=[jax.ShapeDtypeStruct(shape, dtype) for shape, dtype, _ in outs],
+        in_specs=[pl.BlockSpec(memory_space=space) for space in ins],
+        out_specs=[pl.BlockSpec(memory_space=space) for _, _, space in outs],
+        scratch_shapes=scratch,
+        compiler_params=pltpu.CompilerParams(
+            collective_id=collective, has_side_effects=True, vmem_limit_bytes=limit
+        ),
+        name=name,
+    )
+
+
+def forward_call(*operands):
+    any_, vm = pl.ANY, pltpu.VMEM
+    outs = [
+        ((R, D), BF, any_),
+        ((R, D), BF, any_),
+        ((R, D), F32, any_),
+        ((R, D), F32, any_),
+        ((G, D), BF, any_),
+        ((G, D), BF, any_),
+        ((G, F), BF, any_),
+        ((G, F), BF, any_),
+        ((G, 2 * W), BF, any_),
+        ((G, W), BF, any_),
+        ((G, W), BF, any_),
+        ((G, 128), BF, any_),
+        ((3, D, D), BF, any_),
+        ((8, D), F32, vm),
+    ]
+    dma = pltpu.SemaphoreType.DMA
+    scratch = [
+        vm((R, D), BF),
+        vm((R, D), BF),
+        vm((G, 128), BF),
+        vm((3, D, D), BF),
+        vm((D, W), BF),
+        vm((G, D), BF),
+        vm((G, D), BF),
+        vm((G, F), BF),
+        vm((G, F), BF),
+        vm((G, 2 * W), BF),
+        vm((G, W), BF),
+        vm((G, W), BF),
+        vm((R, 3 * W), F32),
+        vm((R, D), F32),
+        vm((R, D), F32),
+        vm((R, D), F32),
+        vm((3, R, D), BF),
+        vm((3, R, D), BF),
+        dma((3, 7)),
+        dma((3, 8)),
+        dma((7,)),
+        dma((7,)),
+        dma((7,)),
+        dma((7,)),
+        dma((3,)),
+        dma((3,)),
+        dma((3,)),
+        dma((3,)),
+        dma((6,)),
+        dma((16,)),
+    ]
+    ins = [any_] * 6 + [vm] * 3
+    return _call(forward_kernel, "forward", outs, ins, scratch, 1, 60 << 20)(*operands)
+
+
+def backward_kernel(
+    tok_h, gz_h, gy_h, mid_h, n1_h, n2_h, act_h, da_h, qk_h, v_h, o_h, aux_h, w_h, vecs, tabs, err,
+    gtok_h, gw_h, small_o,
+    tok, gy, mid, b1, b2, b3, b4, qk, v, o, go, aux, wd, wu, wo, gb, xin, zin, fin, acc, sb, rb,
+    small, stage, came,
+    ns, nr, ms, mr, ts, tr, ps, pr, xs, xr, zs, zr, ss, sr, ls, os_,
+):
+    place = Place()
+    loads = [
+        pltpu.make_async_copy(src, dst, ls.at[i])
+        for i, (src, dst) in enumerate(
+            [
+                (gz_h, b1.at[pl.ds(0, R), :]),
+                (w_h.at[2], wd),
+                (da_h, b3),
+                (act_h, b2),
+                (w_h.at[1], wu),
+                (n2_h, b4),
+                (gy_h, gy),
+                (mid_h, mid),
+                (o_h, o),
+                (qk_h, qk),
+                (v_h, v),
+                (aux_h, aux),
+                (tok_h, tok),
+            ]
+        )
+    ]
+    for copy in loads:
+        copy.start()
+    place.barrier()
+    loads[0].wait()
+    gather = Gather(place, b1, ns, nr)
+    gather.start()
+    small[...] = jnp.zeros_like(small)
+    small[6:7, :] = err[0:1, :]
+    small[5:6, :] = jnp.sum(b1[pl.ds(0, R), :].astype(F32), axis=0, keepdims=True)
+    loads[1].wait()
+    loads[2].wait()
+
+    def column_rows(i, total, r):
+        sub = _rows(32 * i, 32, 32)
+        rows = _rows(R * r + 32 * i, 32, 32)
+        low = (acc[sub, :] * b3[rows, :].astype(F32)).astype(BF)
+        b3[rows, :] = low
+        return total + jnp.sum(low.astype(F32), axis=0, keepdims=True)
+
+    def upper_grad(r, total):
+        @pl.when(r == 1)
+        def _():
+            gather.wait_core()
+
+        @pl.when(r == 2)
+        def _():
+            gather.pass_on()
+
+        @pl.when(r == 3)
+        def _():
+            gather.wait_diagonal()
+
+        acc[...] = _nn(b1[_rows(R * r, R, 128), :], wd[...])
+        return lax.fori_loop(0, R // 32, lambda i, t: column_rows(i, t, r), total)
+
+    up_total = lax.fori_loop(0, 4, upper_grad, jnp.zeros((1, F), F32))
+    small[pl.ds(8 + place.fs, 1), :] = up_total
+
+    far = 1 - lax.div(place.z, 2)
+    near = lax.div(place.z, 2)
+
+    def to_x(chunk, slot, k):
+        rows = _rows(BLK * (2 * place.zs[k] + 1 - place.x), BLK, 32)
+        return _send(gb.at[slot, rows, :], xin.at[chunk, k], xs.at[chunk, k], xr.at[chunk, k], place.xnb)
+
+    def to_z(chunk, slot, k):
+        rows = _rows(BLK * (2 * place.zs[k] + place.x), BLK, 32)
+        return _send(
+            gb.at[slot, rows, :], zin.at[chunk, k - 1], zs.at[chunk, k - 1], zr.at[chunk, k - 1], place.zn[k]
+        )
+
+    def tile(chunk, slot, lhs, rhs, half):
+        rows = _rows(640 * half, 640, 128)
+        gb[slot, rows, :] = _tn(lhs[:, rows], rhs[...]).astype(BF)
+
+    def add_x(chunk, slot, k):
+        to_x(chunk, slot, k).wait_recv()
+        rows = _rows(BLK * (2 * place.zs[k] + place.x), BLK, 32)
+        total = gb[slot, rows, :].astype(F32) + xin[chunk, k].astype(F32)
+        if k == 0:
+            fin[chunk] = total
+        else:
+            gb[slot, rows, :] = total.astype(BF)
+            to_z(chunk, slot, k).start()
+
+    outs = []
+
+    def out(src, dst):
+        copy = pltpu.make_async_copy(src, dst, os_.at[len(outs)])
+        copy.start()
+        outs.append(copy)
+
+    def add_z(chunk, slot):
+        for k in range(1, 4):
+            to_z(chunk, slot, k).wait_recv()
+        fin[chunk] = fin[chunk] + (
+            zin[chunk, 0].astype(F32) + zin[chunk, 1].astype(F32) + zin[chunk, 2].astype(F32)
+        )
+        out(fin.at[chunk], gw_h.at[chunk])
+
+    loads[3].wait()
+    tile(2, 0, b1, b2, far)
+    to_x(2, 0, 2).start()
+    to_x(2, 0, 3).start()
+    tile(2, 0, b1, b2, near)
+    to_x(2, 0, 1).start()
+    to_x(2, 0, 0).start()
+
+    n1_load = pltpu.make_async_copy(n1_h, b2, ls.at[13])
+    n1_load.start()
+    wa_load = pltpu.make_async_copy(w_h.at[0], wd, ls.at[14])
+    wa_load.start()
+
+    loads[4].wait()
+    gather.end()
+    rs1 = Scatter(place, sb, rb, ts, tr)
+
+    def lower_two(t, _):
+        acc[...] = _nt(b3[_rows(R * (3 - t), R, 128), :], wu[...])
+
+        @pl.when(t == 0)
+        def _():
+            rs1.diagonal(acc[...])
+
+        @pl.when(t == 1)
+        def _():
+            rs1.over_y(acc[...])
+
+        @pl.when(t == 2)
+        def _():
+            rs1.other_core(acc[...])
+
+        return 0
+
+    lax.fori_loop(0, 4, lower_two, 0)
+    loads[5].wait()
+    add_x(2, 0, 2)
+    tile(1, 1, b4, b3, far)
+    to_x(1, 1, 2).start()
+    to_x(1, 1, 3).start()
+    add_x(2, 0, 3)
+    tile(1, 1, b4, b3, near)
+    to_x(1, 1, 1).start()
+    to_x(1, 1, 0).start()
+    loads[6].wait()
+    loads[7].wait()
+    rs1.wait()
+    gather2 = Gather(place, b1, ms, mr)
+
+    def norm_rows(i, sums, values, gain, keep):
+        rows = _rows(32 * i, 32, 32)
+        grad = acc[rows, :] + keep.rest(rows)
+        normed, reciprocal = _norm(values[rows, :].astype(F32))
+        scaled = grad * gain
+        back = (
+            scaled
+            - jnp.mean(scaled, axis=-1, keepdims=True)
+            - normed * jnp.mean(scaled * normed, axis=-1, keepdims=True)
+        ) * reciprocal
+        total = gy[rows, :] + back
+        gy[rows, :] = total
+        return (
+            rows,
+            total,
+            (
+                sums[0] + jnp.sum(grad * normed, axis=0, keepdims=True),
+                sums[1] + jnp.sum(grad, axis=0, keepdims=True),
+            ),
+        )
+
+    zero = jnp.zeros((1, D), F32)
+
+    def second_back(i, sums):
+        rows, total, pair = norm_rows(i, sums[:2], mid, vecs[3:4, :], rs1)
+        low = total.astype(BF)
+        b1[rows, :] = low
+        return pair + (sums[2] + jnp.sum(low.astype(F32), axis=0, keepdims=True),)
+
+    gain2, shift2, outb = lax.fori_loop(0, R // 32, second_back, (zero, zero, zero))
+    gather2.start()
+    small[2:3, :] = outb
+    small[3:4, :] = gain2
+    small[4:5, :] = shift2
+    add_x(2, 0, 1)
+    add_x(2, 0, 0)
+    for i in range(8, 12):
+        loads[i].wait()
+    wa_load.wait()
+    wo[...] = wd[:, 3 * W :]
+
+    left = _head_rows(2 * W, 0)
+    right = _head_rows(2 * W, W)
+    side = _head_rows(W, 0)
+
+    def attend_grad(r, total):
+        @pl.when(r == 1)
+        def _():
+            gather2.wait_core()
+
+        @pl.when(r == 2)
+        def _():
+            gather2.pass_on()
+
+        @pl.when(r == 3)
+        def _():
+            gather2.wait_diagonal()
+
+        go[...] = _nn(b1[_rows(R * r, R, 128), :], wo[...]).astype(BF)
+
+        def attend_rows(i, total):
+            mine = _rows(128 * i, 128, 128)
+            rows = _rows(R * r + 128 * i, 128, 128)
+            auxb = aux[rows, :]
+            angle = _nn(auxb, tabs[...])
+            qkb = qk[rows, :]
+            kqb = pltpu.roll(qkb.astype(F32), W, 1).astype(BF)
+            vb = v[rows, :]
+            gob = go[mine, :]
+            keys = _stack(kqb, left)
+            queries = _stack(kqb, right)
+            scores = _nt(qkb, keys) * HD ** (-0.5)
+            probs = _softmax(scores, _allowed(auxb))
+            gprobs = _nt(gob, _stack(vb, side))
+            gscores = []
+            for h in range(HEADS_LOCAL):
+                gp = gprobs[:, 128 * h : 128 * h + 128]
+                delta = jnp.sum(gp * probs[h], axis=-1, keepdims=True)
+                gscores.append((probs[h] * (gp - delta)).astype(BF))
+            flat = jnp.concatenate(gscores, axis=1)
+            tall = jnp.concatenate(gscores, axis=0)
+            ptall = jnp.concatenate([p.astype(BF) for p in probs], axis=0)
+            gqk = (_nn(flat, keys) + _tn(tall, queries)) * HD ** (-0.5)
+            gv = _tn(ptall, _stack(gob, side))
+            turned = (
+                gqk * angle[:, : 2 * W]
+                + pltpu.roll(gqk * angle[:, 4 * W :], 2 * W - 40, 1)
+                + pltpu.roll(gqk * angle[:, 2 * W : 4 * W], 40, 1)
+            )
+            low = jnp.concatenate([turned, gv], axis=1).astype(BF)
+            b3[rows, : 3 * W] = low
+            return total + jnp.sum(low.astype(F32), axis=0, keepdims=True)
+
+        return lax.fori_loop(0, 3, attend_rows, total)
+
+    mix_total = lax.fori_loop(0, 4, attend_grad, jnp.zeros((1, 3 * W), F32))
+    small[pl.ds(12 + place.fs, 1), : 3 * W] = mix_total
+
+    for k in range(4):
+        to_x(2, 0, k).wait_send()
+    for k in range(1, 4):
+        to_z(2, 0, k).wait_send()
+    n1_load.wait()
+
+    def last_tile(half):
+        rows = _rows(640 * half, 640, 128)
+        gb[0, rows, : 3 * W] = _tn(b2[:, rows], b3[:, : 3 * W]).astype(BF)
+        gb[0, rows, 3 * W :] = _tn(b1[:, rows], o[...]).astype(BF)
+
+    last_tile(far)
+    to_x(0, 0, 2).start()
+    to_x(0, 0, 3).start()
+    last_tile(near)
+    to_x(0, 0, 1).start()
+    to_x(0, 0, 0).start()
+    rs1.end()
+    rs2 = Scatter(place, sb, rb, ps, pr)
+
+    def lower_one(t, _):
+        acc[...] = _nt(b3[_rows(R * (3 - t), R, 128), : 3 * W], wd[:, : 3 * W])
+
+        @pl.when(t == 0)
+        def _():
+            rs2.diagonal(acc[...])
+
+        @pl.when(t == 1)
+        def _():
+            rs2.over_y(acc[...])
+
+        @pl.when(t == 2)
+        def _():
+            rs2.other_core(acc[...])
+
+        return 0
+
+    lax.fori_loop(0, 4, lower_one, 0)
+    add_x(1, 1, 2)
+    add_x(1, 1, 3)
+    add_x(1, 1, 1)
+    add_x(1, 1, 0)
+    add_z(2, 0)
+    loads[12].wait()
+    rs2.wait()
+
+    def first_back(i, sums):
+        return norm_rows(i, sums, tok, vecs[0:1, :], rs2)[2]
+
+    gain1, shift1 = lax.fori_loop(0, R // 32, first_back, (zero, zero))
+    out(gy, gtok_h)
+    small[0:1, :] = gain1
+    small[1:2, :] = shift1
+
+    hops = [
+        _send(stage.at[i], came.at[i], ss.at[i], sr.at[i], peer)
+        for i, peer in enumerate((place.core, place.ynb, place.xnb, place.zn[1], place.zn[2]))
+    ]
+    stage[0] = small[...]
+    for i in range(5):
+        hops[i].start()
+        hops[i].wait_recv()
+        total = stage[i] + came[i]
+        if i < 4:
+            stage[i + 1] = total
+        else:
+            small_o[...] = total
+
+    add_z(1, 1)
+    for k in (2, 3, 1, 0):
+        add_x(0, 0, k)
+    add_z(0, 0)
+
+    gather2.end()
+    rs2.end()
+    for hop in hops:
+        hop.wait_send()
+    for chunk, slot in ((1, 1), (0, 0)):
+        for k in range(4):
+            to_x(chunk, slot, k).wait_send()
+        for k in range(1, 4):
+            to_z(chunk, slot, k).wait_send()
+    for copy in outs:
+        copy.wait()
+
+
+def backward_call(*operands):
+    any_, vm = pl.ANY, pltpu.VMEM
+    outs = [((R, D), F32, any_), ((3, BLK, D), F32, any_), ((16, D), F32, vm)]
+    dma = pltpu.SemaphoreType.DMA
+    scratch = [
+        vm((R, D), BF),
+        vm((R, D), F32),
+        vm((R, D), F32),
+        vm((G, D), BF),
+        vm((G, D), BF),
+        vm((G, D), BF),
+        vm((G, D), BF),
+        vm((G, 2 * W), BF),
+        vm((G, W), BF),
+        vm((G, W), BF),
+        vm((R, W), BF),
+        vm((G, 128), BF),
+        vm((D, D), BF),
+        vm((D, D), BF),
+        vm((D, W), BF),
+        vm((2, D, D), BF),
+        vm((3, 4, BLK, D), BF),
+        vm((3, 3, BLK, D), BF),
+        vm((3, BLK, D), F32),
+        vm((R, D), F32),
+        vm((3, R, D), BF),
+        vm((3, R, D), BF),
+        vm((16, D), F32),
+        vm((5, 16, D), F32),
+        vm((5, 16, D), F32),
+        dma((7,)),
+        dma((7,)),
+        dma((7,)),
+        dma((7,)),
+        dma((3,)),
+        dma((3,)),
+        dma((3,)),
+        dma((3,)),
+        dma((3, 4)),
+        dma((3, 4)),
+        dma((3, 3)),
+        dma((3, 3)),
+        dma((5,)),
+        dma((5,)),
+        dma((15,)),
+        dma((8,)),
+    ]
+    ins = [any_] * 13 + [vm] * 3
+    return _call(backward_kernel, "backward", outs, ins, scratch, 2, 64 << 20)(*operands)
+
+
+def turn_tables():
+    import ml_dtypes
+
+    quarter = HD // 4
+    frequency = (1.0 / np.float32(10000.0) ** (np.arange(quarter, dtype=np.float32) * 4.0 / HD)).astype(np.float32)
+    angle = (np.arange(16, dtype=np.float32)[:, None] * frequency[None, :]).astype(np.float32)
+    cosine, sine = np.cos(angle.astype(np.float64)), np.sin(angle.astype(np.float64))
+    zero = np.zeros_like(cosine)
+
+    def head(first, second):
+        top = np.concatenate([first, zero, second, zero], axis=1)
+        low = np.concatenate([zero, first, zero, second], axis=1)
+        return np.tile(np.concatenate([top, low], axis=0), (1, 2 * HEADS_LOCAL))
+
+    full = np.concatenate([head(cosine, cosine), head(-sine, zero), head(zero, sine)], axis=1).astype(np.float32)
+    terms = []
+    rest = full
+    for _ in range(3):
+        term = rest.astype(ml_dtypes.bfloat16)
+        terms.append(term)
+        rest = rest - term.astype(np.float32)
+    terms.append(np.zeros((32, full.shape[1]), ml_dtypes.bfloat16))
+    return jnp.asarray(np.concatenate(terms, axis=0))
+
+
+def row_marks(picture, places, validity):
+    spots = jnp.arange(16, dtype=jnp.int32)
+    row_spot = places[:, 0:1] == spots
+    col_spot = places[:, 1:2] == spots
+    pictures = picture.reshape(-1, ROW_PATCHES)
+    change = (pictures[:, 1:] != pictures[:, :-1]).astype(BF)
+    change = jnp.pad(change, ((0, 0), (1, 0)))
+    upto = jnp.triu(jnp.ones((ROW_PATCHES, ROW_PATCHES), BF))
+    rank = jnp.dot(change, upto, preferred_element_type=F32).reshape(-1, 1)
+    ranks = rank == jnp.arange(8, dtype=F32)
+    once = jnp.concatenate([row_spot, col_spot], axis=1)
+    return jnp.concatenate(
+        [once, once, once, ranks, (validity > 0)[:, None], jnp.zeros((picture.shape[0], 23), bool)], axis=1
+    ).astype(BF)
+
+
+def on_device_fast(
+    tokens,
+    teacher,
+    picture,
+    places,
+    validity,
+    first_gain,
+    first_shift,
+    mixer_weight,
+    mixer_bias,
+    output_weight,
+    output_bias,
+    second_gain,
+    second_shift,
+    upward_weight,
+    upward_bias,
+    downward_weight,
+    downward_bias,
+):
+    member = lax.axis_index("fsdp")
+    data_index = lax.axis_index("dp")
+    data_ways = lax.axis_size("dp")
+    marks = row_marks(picture, places, validity)
+    counts = jnp.sum((validity > 0).astype(F32).reshape(3, ROW_PATCHES), axis=1)
+    vectors = (first_gain, first_shift, output_bias, second_gain, second_shift, downward_bias, upward_bias, mixer_bias)
+    packed = jnp.concatenate(list(vectors) + [jnp.pad(counts.astype(BF), (0, 93))])[None]
+    everyone = lax.all_gather(packed, ("dp", "fsdp"), axis=0, tiled=True)
+    everyone = everyone.reshape(data_ways, lax.axis_size("fsdp"), -1)
+    tally = jnp.sum(everyone[:, :, 2080:2083].astype(F32))
+    factor = 2.0 * ((tokens.shape[0] * data_ways * lax.axis_size("fsdp")) / tally)
+    whole = everyone[:, 0].astype(F32)
+    rows = [whole[:, BLK * i : BLK * (i + 1)].reshape(1, D) for i in range(6)]
+    up_all = whole[:, 960:1600].reshape(4, F)
+    mix_all = whole[:, 1600:2080].reshape(3, 4, W)
+    up_piece = lax.dynamic_slice_in_dim(up_all, member, 1, 0)
+    mix_piece = lax.dynamic_slice_in_dim(mix_all, member, 1, 1).reshape(1, 3 * W)
+    vecs = jnp.concatenate(rows + [up_piece, jnp.full((1, D), factor, F32)], axis=0)
+    wa = jnp.concatenate([mixer_weight.reshape(BLK, 3 * W), output_weight.T], axis=1)
+    tabs = turn_tables()
+    (res, gz, gy, mid, n1, n2, act, da, qk, v, o, aux, w, err) = forward_call(
+        tokens, teacher, marks, wa, upward_weight, downward_weight.T, vecs, mix_piece, tabs
+    )
+    gtok, gw, small = backward_call(
+        tokens, gz, gy, mid, n1, n2, act, da, qk, v, o, aux, w, vecs, tabs, err
+    )
+    pieces = [own_slice(small[i], data_index, data_ways) for i in range(6)]
+    loss = jnp.sum(small[6]) / (tally * D)
+    up_bias = own_slice(small[8:12].reshape(FF), data_index, data_ways)
+    mixed = small[12:16, : 3 * W].reshape(4, 3, W).transpose(1, 0, 2).reshape(3 * D)
+    return (
+        res,
+        loss,
+        gtok,
+        pieces[0],
+        pieces[1],
+        gw[0, :, : 3 * W].reshape(BLK, 3, W),
+        own_slice(mixed[: 2 * D], data_index, data_ways),
+        own_slice(mixed[2 * D :], data_index, data_ways),
+        gw[0, :, 3 * W :].T,
+        pieces[2],
+        pieces[3],
+        pieces[4],
+        gw[1],
+        up_bias,
+        gw[2].T,
+        pieces[5],
+    )
+
+
 def solution(mesh):
+    fast = mesh.shape["dp"] == 8 and mesh.shape["fsdp"] == 4
     return jax.shard_map(
-        on_device,
+        on_device_fast if fast else on_device,
         mesh=mesh,
         in_specs=(
             P(("dp", "fsdp"), None),

time: 1220 us -> 440 us (0.36)
  waiting for transfers between devices: 614 us -> 0 us
  Pallas kernels: 0 us -> 359 us
  blocking collectives: 232 us -> 44 us
  matrix products: 145 us -> 0.2 us
  local copies, waits for them, and re-layouts: 106 us -> 22.1 us
  other arithmetic: 87.7 us -> 6.73 us
  between operations: 24 us -> 4.23 us
    reduce_scatter x16 -> x0, waiting for transfers between devices: 371 us -> none  [the longest x3 85.1 us: on_device(): lax.psum_scatter(jnp.einsum('re,de->rd', grad_mixed, mixer_flat, preferre...]
    pallas_call x0 -> x2, Pallas kernels: none -> 359 us  [the longest x1 188 us: backward_call(): _call(backward_kernel, 'backward', outs, ins, scratch, 2, 64 << 20)]
    all_gather x15 -> x0, waiting for transfers between devices: 240 us -> none  [the longest x1 58.5 us: on_device(): lax.all_gather(downward_weight, 'dp', axis=1, tiled=True)]
    dot_general x54 -> x1, matrix products: 145 us -> 0.2 us  [row_marks(): rank = jnp.dot(change, upto, preferred_element_type=F32).reshape(-1, 1)]
    psum x2 -> x0, blocking collectives: 82.4 us -> none  [the longest x1 43.1 us: on_device(): lax.psum((small_sums[0], small_sums[1], small_sums[2], small_sums[3], sma...]
    all_gather x11 -> x1, blocking collectives: 109 us -> 44 us  [on_device_fast(): everyone = lax.all_gather(packed, ('dp', 'fsdp'), axis=0, tiled=True)]
    unnamed x1 -> x0, blocking collectives: 40.7 us -> none
    reduce_sum x20 -> x2, other arithmetic: 32.2 us -> 1.48 us  [the longest x1 0.8 us: on_device_fast(): counts = jnp.sum((validity > 0).astype(F32).reshape(3, ROW_PATCHES), axis=1)]
  transfers between devices with their start and end apart: 31 -> 0, of which waited for: 25 -> 0; matrix products, arithmetic and copies ran while one was open for 22% -> 0% of each run, Pallas kernels for 0% -> 0%
where the time goes in v1:
time: 440 us; the launch traced here: 436 us
  Pallas kernels  359 us (82%)
  blocking collectives  44 us (10%)
  local copies, waits for them, and re-layouts  22.1 us (5%)
  other arithmetic  6.73 us (2%)
    pallas_call x1, Pallas kernels, backward_call(): _call(backward_kernel, 'backward', outs, ins, scratch, 2, 64 << 20)  188 us
    pallas_call x1, Pallas kernels, forward_call(): _call(forward_kernel, 'forward', outs, ins, scratch, 1, 60 << 20)(*operands)  170 us
    all_gather x1, blocking collectives, on_device_fast(): everyone = lax.all_gather(packed, ('dp', 'fsdp'), axis=0, tiled=True)  44 us

profile of v1, /device:TPU:0, one launch (start us, length us, event | category | flops | bytes accessed | tf_op | source)
XLA Modules:
  0.0 436.0 jit_solution(14296368586478447077)
XLA Ops:
  0.7 0.0 copy-start.3
  0.7 0.0 copy-start.6
  0.7 0.0 copy-start.7
  0.7 0.0 copy-start.8
  0.7 0.0 copy-start.9
  0.7 0.0 copy-start.10
  0.7 0.0 copy-start.11
  0.7 0.0 copy-start.4
  0.7 0.0 copy-start.5
  0.7 0.8 slice_reduce_fusion.2
  1.6 0.2 iota_compare_fusion.1
  1.7 0.8 slice_compare_fusion
  2.6 0.2 convolution_bitcast_fusion
  2.8 0.1 iota_compare_fusion
  2.9 0.8 bitcast_reduce_fusion
  3.7 0.1 broadcast_in_dim.28
  3.9 0.5 concatenate.14
  4.4 0.7 convert_element_type.21.aux_h
  5.0 1.2 copy.48
  6.3 0.3 reshape.94
  6.6 0.0 copy-done.3
  6.6 0.9 pad_maximum_fusion.wa_h
  7.5 0.0 copy-done.6
  7.6 0.1 concatenate.16
  7.7 44.0 %all-gather.1 = bf16[32,1,2176]{2,1,0:T(2,128)(2,1)S(1)} all-gather(bf16[1,1,2176]{2,1,0:T(2,128)(2,1)S(1)} %reshape.114), channel_id=2, replica_groups=mesh['dp'=8,'fsdp'=4] {'dp','fsdp'}, dimensions={0}, use_global_device_ids=true | all-gather | bytes 143616 | tf_op jit(solution)/shard_map/all_gather | solution.py:1364
  51.7 0.8 reduce.3
  52.5 0.1 fusion.10
  52.6 0.1 reshape.98
  52.7 0.1 reshape.99
  52.8 0.1 reshape.100
  52.9 0.1 reshape.101
  53.0 0.1 reshape.102
  53.0 0.1 reshape.103
  53.1 0.1 slice.131
  53.2 0.7 convert_reduce_fusion
  54.6 0.7 concatenate.17.vecs
  55.3 0.1 slice.133
  55.4 0.1 reshape.105
  55.5 0.7 reshape.106.mixb
  56.2 170.4 %forward.1 = (bf16[384,1280]{1,0:T(8,128)(2,1)}, bf16[384,1280]{1,0:T(8,128)(2,1)}, f32[384,1280]{1,0:T(8,128)}, f32[384,1280]{1,0:T(8,128)}, bf16[1536,1280]{1,...) custom-call(bf16[384,1280]{1,0:T(8,128)(2,1)} %tok_h.3, ...), custom_call_target="tpu_custom_call" | custom-call | tf_op jit(solution)/shard_map/forward/pallas_call | solution.py:902
  226.6 188.5 %backward.1 = (f32[384,1280]{1,0:T(8,128)}, f32[3,160,1280]{2,1,0:T(8,128)}, f32[16,1280]{1,0:T(8,128)}) custom-call(bf16[384,1280]{1,0:T(8,128)(2,1)} %tok_h.3, bf16[384,1280]{1,0:T(8,128)(2,1)} %get-tuple-element.34.gz_h, f32[384,1280]{1,0:T(8,128)} %get-tuple-element.35.gy_h, f32[384,1280]{1,0:T(8,128)} %get-tuple-element.36.mid_h, ...), custom_call_target="tpu_custom_call" | custom-call | tf_op jit(solution)/shard_map/backward/pallas_call | solution.py:1294
  415.0 1.8 fusion.9
  418.3 0.6 constant_dynamic-slice_fusion.5
  418.9 0.6 constant_dynamic-slice_fusion.4
  419.6 2.0 slice.110
  421.5 1.5 reshape_squeeze.3
  423.1 0.9 copy.51
  424.0 0.8 slice.111
  424.8 0.1 reshape.107
  424.9 0.1 slice.113
  425.0 0.7 dynamic_slice.51
  425.7 0.1 slice.115
  425.8 0.6 dynamic_slice.52
  426.4 0.0 copy-done
  426.4 0.8 slice_bitcast_fusion.2
  427.3 0.6 constant_dynamic-slice_fusion.3
  427.9 0.6 constant_dynamic-slice_fusion.2
  428.5 0.6 constant_dynamic-slice_fusion.1
  429.2 1.3 slice_bitcast_fusion
  430.4 0.9 slice.121
  431.4 0.7 dynamic_slice.59
  432.0 0.6 constant_dynamic-slice_fusion
  432.7 0.9 copy.59
  433.6 1.3 copy.60
  (27 shorter events, 0.3 us)
Async XLA Ops:
  0.7 6.0 %copy-start.3 = (bf16[320,160]{0,1:T(8,128)(2,1)S(1)}, bf16[320,160]{0,1:T(8,128)(2,1)}, u32[]{:S(2)}) copy-start(bf16[320,160]{0,1:T(8,128)(2,1)} %param.27) | copy-start | bytes 307204
  0.7 6.8 %copy-start.6 = (bf16[160]{0:T(256)(128)(2,1)S(1)}, bf16[160]{0:T(256)(128)(2,1)}, u32[]{:S(2)}) copy-start(bf16[160]{0:T(256)(128)(2,1)} %param.23) | copy-start | bytes 964
  0.7 6.8 %copy-start.7 = (bf16[160]{0:T(256)(128)(2,1)S(1)}, bf16[160]{0:T(256)(128)(2,1)}, u32[]{:S(2)}) copy-start(bf16[160]{0:T(256)(128)(2,1)} %param.24) | copy-start | bytes 964
  0.7 6.8 %copy-start.8 = (bf16[160]{0:T(256)(128)(2,1)S(1)}, bf16[160]{0:T(256)(128)(2,1)}, u32[]{:S(2)}) copy-start(bf16[160]{0:T(256)(128)(2,1)} %param.28) | copy-start | bytes 964
  0.7 6.8 %copy-start.9 = (bf16[160]{0:T(256)(128)(2,1)S(1)}, bf16[160]{0:T(256)(128)(2,1)}, u32[]{:S(2)}) copy-start(bf16[160]{0:T(256)(128)(2,1)} %param.29) | copy-start | bytes 964
  0.7 6.8 %copy-start.10 = (bf16[160]{0:T(256)(128)(2,1)S(1)}, bf16[160]{0:T(256)(128)(2,1)}, u32[]{:S(2)}) copy-start(bf16[160]{0:T(256)(128)(2,1)} %param.30) | copy-start | bytes 964
  0.7 6.8 %copy-start.11 = (bf16[160]{0:T(256)(128)(2,1)S(1)}, bf16[160]{0:T(256)(128)(2,1)}, u32[]{:S(2)}) copy-start(bf16[160]{0:T(256)(128)(2,1)} %param.34) | copy-start | bytes 964
  0.7 6.8 %copy-start.4 = (bf16[640]{0:T(1024)(128)(2,1)S(1)}, bf16[640]{0:T(1024)(128)(2,1)}, u32[]{:S(2)}) copy-start(bf16[640]{0:T(1024)(128)(2,1)} %param.32) | copy-start | bytes 3844
  0.7 6.8 %copy-start.5 = (bf16[480]{0:T(512)(128)(2,1)S(1)}, bf16[480]{0:T(512)(128)(2,1)}, u32[]{:S(2)}) copy-start(bf16[480]{0:T(512)(128)(2,1)} %param.26) | copy-start | bytes 2884
  416.8 9.6 %copy-start = (f32[3,160,1280]{2,1,0:T(8,128)S(1)}, f32[3,160,1280]{2,1,0:T(8,128)}, u32[]{:S(2)}) copy-start(f32[3,160,1280]{2,1,0:T(8,128)} %get-tuple-element.49) | copy-start | bytes 7372804
  424.0 8.7 %copy-start.2 = (bf16[384,1280]{1,0:T(8,128)(2,1)S(1)}, bf16[384,1280]{1,0:T(8,128)(2,1)}, u32[]{:S(2)}) copy-start(bf16[384,1280]{1,0:T(8,128)(2,1)} %get-tuple-element.151) | copy-start | bytes 2949124
  430.4 3.2 copy-start.1

commit v2 on v0

--- a/solution.py
+++ b/solution.py
@@ -1,6 +1,9 @@
+import numpy as np
 import jax
 import jax.numpy as jnp
 from jax import lax
+from jax.experimental import pallas as pl
+from jax.experimental.pallas import tpu as pltpu
 from jax.sharding import PartitionSpec as P
 
 D = 1280
@@ -384,9 +387,970 @@
     )
 
 
+BF = jnp.bfloat16
+F32 = jnp.float32
+HEADS_LOCAL = 4
+W = 320
+F = 1280
+R = 384
+G = 1536
+BLK = 160
+SUB = 128
+QUAD = 512
+HALF = 640
+MESH_ID = pl.DeviceIdType.MESH
+
+
+def _nn(a, b):
+    return lax.dot_general(a, b, (((1,), (0,)), ((), ())), preferred_element_type=F32)
+
+
+def _nt(a, b):
+    return lax.dot_general(a, b, (((1,), (1,)), ((), ())), preferred_element_type=F32)
+
+
+def _tn(a, b):
+    return lax.dot_general(a, b, (((0,), (0,)), ((), ())), preferred_element_type=F32)
+
+
+def _ds(start, size, step):
+    if isinstance(start, int):
+        return pl.ds(start, size)
+    return pl.ds(pl.multiple_of(start, step), size)
+
+
+class Place:
+    def __init__(self):
+        dp = lax.axis_index("dp")
+        fs = lax.axis_index("fsdp")
+        z, x = lax.div(dp, 2), lax.rem(dp, 2)
+        y, c = lax.div(fs, 2), lax.rem(fs, 2)
+        self.z, self.x, self.fs, self.dp = z, x, fs, dp
+        self.core = (dp, 2 * y + 1 - c)
+        self.ynb = (dp, 2 * (1 - y) + c)
+        self.xnb = (2 * z + 1 - x, fs)
+        self.zs = (z, z + 1 - 2 * lax.rem(z, 2), lax.rem(z + 2, 4), 3 - z)
+        self.zn = tuple((2 * zk + x, fs) for zk in self.zs)
+        self.up = (2 * jnp.minimum(z + 1, 3) + x, fs)
+        self.down = (2 * jnp.maximum(z - 1, 0) + x, fs)
+        self.near = lax.div(z, 2)
+        self.far = 1 - self.near
+
+    def barrier(self):
+        sem = pltpu.get_barrier_semaphore()
+        for peer in (self.core, self.ynb, self.xnb) + self.zn[1:]:
+            pl.semaphore_signal(sem, inc=1, device_id=peer, device_id_type=MESH_ID)
+        pl.semaphore_wait(sem, 6)
+
+
+def _send(src, dst, ss, rs, peer):
+    return pltpu.make_async_remote_copy(
+        src_ref=src, dst_ref=dst, send_sem=ss, recv_sem=rs, device_id=peer, device_id_type=MESH_ID
+    )
+
+
+class Gather:
+    def __init__(self, place, buf, ss, rs, cols=slice(None)):
+        self.place, self.buf, self.ss, self.rs, self.cols = place, buf, ss, rs, cols
+
+    def part(self, s, slot):
+        return self.buf.at[_ds(QUAD * s + SUB * slot, SUB, SUB), self.cols]
+
+    def to_core(self, s):
+        return _send(self.part(s, 0), self.part(s, 1), self.ss.at[s], self.rs.at[s], self.place.core)
+
+    def to_y(self, s):
+        return _send(self.part(s, 0), self.part(s, 2), self.ss.at[3 + s], self.rs.at[3 + s], self.place.ynb)
+
+    def on(self, s):
+        return _send(self.part(s, 2), self.part(s, 3), self.ss.at[6 + s], self.rs.at[6 + s], self.place.core)
+
+    def start(self, s):
+        self.to_y(s).start()
+        self.to_core(s).start()
+
+    def pass_on(self, s):
+        self.to_y(s).wait_recv()
+        self.on(s).start()
+
+    def ready(self, s):
+        self.to_core(s).wait_recv()
+        self.on(s).wait_recv()
+
+    def end(self):
+        for s in range(3):
+            self.to_core(s).wait_send()
+            self.to_y(s).wait_send()
+            self.on(s).wait_send()
+
+
+class Scatter:
+    def __init__(self, place, sb, rb, own, ss, rs, cols=slice(None)):
+        self.place, self.sb, self.rb, self.own, self.ss, self.rs, self.cols = place, sb, rb, own, ss, rs, cols
+
+    def copy(self, kind, s):
+        peer = self.place.ynb if kind == 1 else self.place.core
+        slot = 2 + s if kind == 1 else kind // 2
+        return _send(
+            self.sb.at[slot, :, self.cols],
+            self.rb.at[kind, s, :, self.cols],
+            self.ss.at[3 * kind + s],
+            self.rs.at[3 * kind + s],
+            peer,
+        )
+
+    def again(self, kind, s):
+        if isinstance(s, int):
+            if s > 0:
+                self.copy(kind, s - 1).wait_send()
+        else:
+            pl.when(s > 0)(lambda: self.copy(kind, s - 1).wait_send())
+
+    def post(self, s, lhs, rhs):
+        rows = QUAD * s
+        term = _nt(lhs(_ds(rows + 2 * SUB, 2 * SUB, SUB)), rhs())
+        self.again(0, s)
+        self.sb[0, :, self.cols] = term[SUB:].astype(BF)
+        self.copy(0, s).start()
+        mine = _nt(lhs(_ds(rows, 2 * SUB, SUB)), rhs())
+        self.again(2, s)
+        self.sb[1, :, self.cols] = mine[SUB:].astype(BF)
+        self.copy(2, s).start()
+        self.own[_ds(SUB * s, SUB, SUB), self.cols] = mine[:SUB]
+        self.copy(0, s).wait_recv()
+        self.sb[2 + s, :, self.cols] = (term[:SUB] + self.rb[0, s, :, self.cols].astype(F32)).astype(BF)
+        self.copy(1, s).start()
+
+    def wait(self, s):
+        self.copy(2, s).wait_recv()
+        self.copy(1, s).wait_recv()
+
+    def total(self, s, i, step):
+        sub = _ds(step * i, step, step)
+        return self.own[_ds(SUB * s + step * i, step, step), self.cols] + (
+            self.rb[2, s, sub, self.cols].astype(F32) + self.rb[1, s, sub, self.cols].astype(F32)
+        )
+
+    def end(self):
+        self.copy(0, 2).wait_send()
+        self.copy(2, 2).wait_send()
+        for s in range(3):
+            self.copy(1, s).wait_send()
+
+
+def _norm(values):
+    average = jnp.mean(values, axis=-1, keepdims=True)
+    centered = values - average
+    reciprocal = lax.rsqrt(jnp.mean(centered * centered, axis=-1, keepdims=True) + EPSILON)
+    return centered * reciprocal, reciprocal
+
+
+def _head_rows(lanes, offset):
+    lane = lax.broadcasted_iota(jnp.int32, (1, lanes), 1) - offset
+    return [
+        jnp.where((lane >= HD * h) & (lane < HD * h + HD), 1.0, 0.0).astype(BF)
+        for h in range(HEADS_LOCAL)
+    ]
+
+
+def _stack(values, heads):
+    return jnp.concatenate([values * head for head in heads], axis=0)
+
+
+def _allowed(auxb):
+    lane = lax.broadcasted_iota(jnp.int32, (1, 128), 1)
+    picks = (lane >= 96) & (lane < 104)
+    left = jnp.where(picks, auxb.astype(F32), jnp.where(lane == 104, 1.0, 0.0)).astype(BF)
+    score = _nt(left, auxb)
+    here = lax.broadcasted_iota(jnp.int32, (128, 128), 0)
+    there = lax.broadcasted_iota(jnp.int32, (128, 128), 1)
+    return (score > 1.5) | (here == there)
+
+
+def _softmax(scores, allowed):
+    probs = []
+    for h in range(HEADS_LOCAL):
+        part = jnp.where(allowed, scores[:, 128 * h : 128 * h + 128], -1e30)
+        grown = jnp.exp(part - jnp.max(part, axis=-1, keepdims=True))
+        probs.append(grown * (1.0 / jnp.sum(grown, axis=-1, keepdims=True)))
+    return probs
+
+
+PIECES = ((0, 0, 1024), (0, 1024, 256), (1, 0, 1280), (2, 0, 1280))
+
+
+def layer_kernel(
+    tok_h, teach_h, aux_h, wa_h, wu_h, wd_h, sv, tabs,
+    res_h, gtok_h, gw_h, small_o, loss_o, keep_h,
+    tok, aux, w, wo, n1a, n2, gu, gzb, qk, v, o, acc, own, mid, gy, sb, rb,
+    gb, xin, zin, fin, vecs, cst, cca, small, stage, came,
+    ws, wr, ags, agr, rss, rsr, vs, vr, cs, cr, xs, xr, zs, zr, ss, sr, ls, os_, xfree, zfree, gfree,
+):
+    place = Place()
+    z, x = place.z, place.x
+    patches = TOTAL[0]
+    mine = _ds(BLK * (2 * z + x), BLK, 32)
+    loads = [
+        pltpu.make_async_copy(src, dst, ls.at[i])
+        for i, (src, dst) in enumerate(
+            [(tok_h, tok)]
+            + [(aux_h.at[pl.ds(SUB * s, SUB), :], aux.at[pl.ds(QUAD * s, SUB), :]) for s in range(3)]
+            + [(wa_h, w.at[0, mine, :]), (wu_h, w.at[1, mine, :]), (wd_h, w.at[2, mine, :])]
+        )
+    ]
+    for copy in loads:
+        copy.start()
+    place.barrier()
+
+    shards = (wa_h, wu_h, wd_h)
+
+    def at(piece, zk, xk):
+        third, start, size = PIECES[piece]
+        return w.at[third, _ds(BLK * (2 * zk + xk), BLK, 32), pl.ds(start, size)]
+
+    def shard(piece):
+        third, start, size = PIECES[piece]
+        return shards[third].at[:, pl.ds(start, size)]
+
+    def first(piece, i):
+        peer = (place.xnb, place.up, place.down)[i]
+        return _send(shard(piece), at(piece, z, x), ws.at[piece, i], wr.at[piece, 2 * z + x], peer)
+
+    def begin_z(piece):
+        pl.when(z < 3)(lambda: first(piece, 1).start())
+        pl.when(z > 0)(lambda: first(piece, 2).start())
+
+    def begin_x(piece):
+        first(piece, 0).start()
+
+    def hop(piece, d, i):
+        zk = jnp.maximum(z - d, 0) if i < 2 else jnp.minimum(z + d, 3)
+        peer = (place.up, place.xnb, place.down, place.xnb)[i]
+        there = at(piece, zk, x)
+        return _send(there, there, ws.at[piece, 4 * d - 1 + i], wr.at[piece, 2 * zk + x], peer)
+
+    def relay(piece, d):
+        @pl.when(z >= d)
+        def _():
+            hop(piece, d, 0).wait_recv()
+            pl.when(z < 3)(lambda: hop(piece, d, 0).start())
+            hop(piece, d, 1).start()
+
+        @pl.when(z + d <= 3)
+        def _():
+            hop(piece, d, 2).wait_recv()
+            pl.when(z > 0)(lambda: hop(piece, d, 2).start())
+            hop(piece, d, 3).start()
+
+    def over_x(piece, zk):
+        there = at(piece, zk, 1 - x)
+        _send(there, there, ws.at[piece, 0], wr.at[piece, 2 * zk + 1 - x], place.xnb).wait_recv()
+
+    def complete(piece):
+        for k in range(4):
+            over_x(piece, place.zs[k])
+
+    def sent(piece):
+        first(piece, 0).wait_send()
+        pl.when(z < 3)(lambda: first(piece, 1).wait_send())
+        pl.when(z > 0)(lambda: first(piece, 2).wait_send())
+        for d in range(1, 4):
+
+            @pl.when(z >= d)
+            def _(d=d):
+                pl.when(z < 3)(lambda: hop(piece, d, 0).wait_send())
+                hop(piece, d, 1).wait_send()
+
+            @pl.when(z + d <= 3)
+            def _(d=d):
+                pl.when(z > 0)(lambda: hop(piece, d, 2).wait_send())
+                hop(piece, d, 3).wait_send()
+
+    outs = []
+
+    def out(src, dst):
+        copy = pltpu.make_async_copy(src, dst, os_.at[len(outs)])
+        copy.start()
+        outs.append(copy)
+        return len(outs) - 1
+
+    begin_z(0)
+    begin_x(0)
+
+    vector_hops = [
+        _send(stage.at[i, pl.ds(0, 8), :], came.at[i, pl.ds(0, 8), :], vs.at[i], vr.at[i], peer)
+        for i, peer in enumerate((place.xnb, place.zn[1], place.zn[2]))
+    ]
+    stage[0, :8, :] = sv[...]
+    agx = Gather(place, aux, ags.at[1], agr.at[1])
+    for i in range(3):
+        vector_hops[i].start()
+        loads[1 + i].wait()
+        agx.start(i)
+        vector_hops[i].wait_recv()
+        total = stage[i, :8, :] + came[i, :8, :]
+        if i < 2:
+            stage[i + 1, :8, :] = total
+        else:
+            vecs[...] = total
+
+    loads[0].wait()
+    ag1 = Gather(place, n1a, ags.at[0], agr.at[0])
+
+    def first_norm(i, s):
+        rows = _ds(QUAD * s + 32 * i, 32, 32)
+        normed, _r = _norm(tok[_ds(SUB * s + 32 * i, 32, 32), :].astype(F32))
+        n1a[rows, :] = (normed * vecs[0:1, :] + vecs[1:2, :]).astype(BF)
+        return s
+
+    for s in range(3):
+        lax.fori_loop(0, 4, first_norm, s)
+        ag1.start(s)
+    relay(0, 1)
+    begin_z(1)
+    for s in range(3):
+        agx.pass_on(s)
+    ag1.pass_on(0)
+    ag1.pass_on(1)
+    relay(0, 2)
+    begin_z(2)
+    for s in range(3):
+        agx.ready(s)
+
+    count_hops = [
+        _send(cst.at[i], cca.at[i], cs.at[i], cr.at[i], peer)
+        for i, peer in enumerate((place.xnb, place.zn[1], place.zn[2]))
+    ]
+    cst[0] = _nn(jnp.ones((8, G), BF), aux[...])
+    count_hops[0].start()
+    ag1.pass_on(2)
+    count_hops[0].wait_recv()
+    cst[1] = cst[0] + cca[0]
+    count_hops[1].start()
+    relay(0, 3)
+    begin_x(1)
+    relay(1, 1)
+    count_hops[1].wait_recv()
+    cst[2] = cst[1] + cca[1]
+    count_hops[2].start()
+    relay(1, 2)
+    relay(1, 3)
+    begin_x(2)
+    count_hops[2].wait_recv()
+    real_count = (cst[2] + cca[2])[0:1, 104:105]
+    complete(0)
+    loads[4].wait()
+
+    left = _head_rows(2 * W, 0)
+    right = _head_rows(2 * W, W)
+    side = _head_rows(W, 0)
+    rs1 = Scatter(place, sb, rb, own, rss.at[0], rsr.at[0])
+
+    def attend_part(s, _):
+        ag1.ready(s)
+        acc[:, : 3 * W] = _nn(n1a[_ds(QUAD * s, QUAD, QUAD), :], w[0, :, : 3 * W]) + vecs[7:8, : 3 * W]
+
+        def attend_rows(i, _):
+            here = _ds(SUB * i, SUB, SUB)
+            rows = _ds(QUAD * s + SUB * i, SUB, SUB)
+            auxb = aux[rows, :]
+            angle = _nn(auxb, tabs[...])
+            raw = acc[here, : 2 * W]
+            turned = (
+                raw * angle[:, : 2 * W]
+                + pltpu.roll(raw, 2 * W - 40, 1) * angle[:, 2 * W : 4 * W]
+                + pltpu.roll(raw, 40, 1) * angle[:, 4 * W :]
+            )
+            qkb = turned.astype(BF)
+            kqb = pltpu.roll(turned, W, 1).astype(BF)
+            vb = acc[here, 2 * W : 3 * W].astype(BF)
+            qk[rows, :] = qkb
+            v[rows, :] = vb
+            scores = _nt(qkb, _stack(kqb, left)) * HD ** (-0.5)
+            probs = _softmax(scores, _allowed(auxb))
+            flat = jnp.concatenate([p.astype(BF) for p in probs], axis=1)
+            o[rows, :] = _nn(flat, _stack(vb, side)).astype(BF)
+            return 0
+
+        lax.fori_loop(0, 4, attend_rows, 0)
+
+        @pl.when(s == 0)
+        def _():
+            complete(1)
+            wo[...] = w[0, :, 3 * W :]
+            relay(2, 1)
+
+        rs1.post(s, lambda rows: o[rows, :], lambda: wo[...])
+
+        @pl.when(s == 1)
+        def _():
+            relay(2, 2)
+            begin_z(3)
+
+        return 0
+
+    lax.fori_loop(0, 3, attend_part, 0)
+    n1_kept = out(n1a, keep_h)
+    ag2 = Gather(place, n2, ags.at[2], agr.at[2])
+
+    def second_norm(s, _):
+        rs1.wait(s)
+
+        def rows_of(i, _):
+            rows = _ds(SUB * s + 32 * i, 32, 32)
+            middle = tok[rows, :].astype(F32) + rs1.total(s, i, 32) + vecs[2:3, :]
+            mid[rows, :] = middle
+            normed, _r = _norm(middle)
+            n2[_ds(QUAD * s + 32 * i, 32, 32), :] = (normed * vecs[3:4, :] + vecs[4:5, :]).astype(BF)
+            return 0
+
+        lax.fori_loop(0, 4, rows_of, 0)
+        ag2.start(s)
+
+        @pl.when(s == 0)
+        def _():
+            relay(2, 3)
+            begin_x(3)
+
+        return 0
+
+    lax.fori_loop(0, 3, second_norm, 0)
+    teach = tok
+    teach_load = pltpu.make_async_copy(teach_h, teach, ls.at[7])
+    teach_load.start()
+    relay(3, 1)
+    ag1.end()
+    outs[n1_kept].wait()
+    loads[5].wait()
+    complete(2)
+
+    def up_part(s, _):
+        ag2.pass_on(s)
+        ag2.ready(s)
+        acc[...] = _nn(n2[_ds(QUAD * s, QUAD, QUAD), :], w[1]) + vecs[6:7, :]
+
+        def rows_of(i, _):
+            upper = acc[_ds(32 * i, 32, 32), :]
+            rows = _ds(QUAD * s + 32 * i, 32, 32)
+            gate = 1.0 / (1.0 + jnp.exp(-1.702 * upper))
+            n1a[rows, :] = (upper * gate).astype(BF)
+            gu[rows, :] = (gate + 1.702 * upper * gate * (1.0 - gate)).astype(BF)
+            return 0
+
+        lax.fori_loop(0, QUAD // 32, rows_of, 0)
+        return 0
+
+    lax.fori_loop(0, 3, up_part, 0)
+    act = n1a
+    relay(3, 2)
+    rs1.end()
+    loads[6].wait()
+    teach_load.wait()
+
+    cols = {0: _ds(HALF * place.near, HALF, 128), 1: _ds(HALF * place.far, HALF, 128)}
+    factor = 2.0 * patches / real_count
+    downs = [Scatter(place, sb, rb, own, rss.at[1 + j], rsr.at[1 + j], cols[j]) for j in range(2)]
+    gathers = [Gather(place, gzb, ags.at[3 + j], agr.at[3 + j], cols[j]) for j in range(2)]
+    small[...] = jnp.zeros_like(small)
+
+    for j in range(2):
+        for k in ((0, 1), (2, 3))[j]:
+            over_x(3, place.zs[k])
+        half = (place.near, place.far)[j]
+
+        def down_part(s, _, j=j, half=half):
+            downs[j].post(s, lambda rows: act[rows, :], lambda: w[2, _ds(HALF * half, HALF, 128), :])
+            return 0
+
+        lax.fori_loop(0, 3, down_part, 0)
+
+        def finish_part(s, sums, j=j):
+            downs[j].wait(s)
+
+            def rows_of(i, sums):
+                rows = _ds(SUB * s + 32 * i, 32, 32)
+                result = mid[rows, cols[j]] + downs[j].total(s, i, 32) + vecs[5:6, cols[j]]
+                real = aux[_ds(QUAD * s + 32 * i, 32, 32), 104:105].astype(F32)
+                difference = result - teach[rows, cols[j]].astype(F32)
+                masked = real * difference
+                gout = factor * masked
+                low = gout.astype(BF)
+                gy[rows, cols[j]] = gout
+                teach[rows, cols[j]] = result.astype(BF)
+                gzb[_ds(QUAD * s + 32 * i, 32, 32), cols[j]] = low
+                return (
+                    sums[0] + jnp.sum(masked * difference, axis=0, keepdims=True),
+                    sums[1] + jnp.sum(low.astype(F32), axis=0, keepdims=True),
+                )
+
+            sums = lax.fori_loop(0, 4, rows_of, sums)
+            gathers[j].start(s)
+            if j == 0:
+                pl.when(s == 1)(lambda: relay(3, 3))
+            else:
+                gathers[0].pass_on(s)
+            return sums
+
+        zero = jnp.zeros((1, HALF), F32)
+        sums = lax.fori_loop(0, 3, finish_part, (zero, zero))
+        small[6:7, cols[j]] = sums[0]
+        small[5:6, cols[j]] = sums[1]
+    res_out = out(teach, res_h)
+
+    def to_x(chunk, slot, k):
+        rows = _ds(BLK * (2 * place.zs[k] + 1 - x), BLK, 32)
+        return _send(gb.at[slot, rows, :], xin.at[slot, k], xs.at[chunk, k], xr.at[chunk, k], place.xnb)
+
+    def to_z(chunk, slot, k):
+        rows = _ds(BLK * (2 * place.zs[k] + x), BLK, 32)
+        return _send(
+            gb.at[slot, rows, :], zin.at[slot, k - 1], zs.at[chunk, k - 1], zr.at[chunk, k - 1], place.zn[k]
+        )
+
+    def tile(slot, lhs, rhs, half):
+        rows = _ds(HALF * half, HALF, 128)
+        for part in range(2):
+            cols = pl.ds(HALF * part, HALF)
+            gb[slot, rows, cols] = _tn(lhs[:, rows], rhs[:, cols]).astype(BF)
+
+    def add_x(chunk, slot, k):
+        to_x(chunk, slot, k).wait_recv()
+        rows = _ds(BLK * (2 * place.zs[k] + x), BLK, 32)
+        gb[slot, rows, :] = (gb[slot, rows, :].astype(F32) + xin[slot, k].astype(F32)).astype(BF)
+        to_z(chunk, slot, k).start()
+
+    def add_z(chunk, slot):
+        to_x(chunk, slot, 0).wait_recv()
+        for k in range(1, 4):
+            to_z(chunk, slot, k).wait_recv()
+
+        def rows_of(i, _):
+            rows = _ds(32 * i, 32, 32)
+            kept = _ds(BLK * (2 * z + x) + 32 * i, 32, 32)
+            fin[rows, :] = (gb[slot, kept, :].astype(F32) + xin[slot, 0, rows, :].astype(F32)) + (
+                zin[slot, 0, rows, :].astype(F32)
+                + zin[slot, 1, rows, :].astype(F32)
+                + zin[slot, 2, rows, :].astype(F32)
+            )
+            return 0
+
+        lax.fori_loop(0, BLK // 32, rows_of, 0)
+        return out(fin, gw_h.at[chunk])
+
+    for s in range(3):
+        gathers[0].ready(s)
+    tile(0, gzb, act, place.near)
+    to_x(2, 0, 1).start()
+    to_x(2, 0, 0).start()
+
+    for copy in downs:
+        copy.end()
+    rs3 = Scatter(place, sb, rb, own, rss.at[3], rsr.at[3])
+    up_total = jnp.zeros((1, F), F32)
+    for s in range(3):
+        gathers[1].pass_on(s)
+    gathers[1].ready(0)
+    for s in range(3):
+        acc[...] = _nn(gzb[pl.ds(QUAD * s, QUAD), :], w[2])
+
+        def gate_rows(i, total, s=s):
+            rows = _ds(QUAD * s + 32 * i, 32, 32)
+            low = (acc[_ds(32 * i, 32, 32), :] * gu[rows, :].astype(F32)).astype(BF)
+            gu[rows, :] = low
+            return total + jnp.sum(low.astype(F32), axis=0, keepdims=True)
+
+        up_total = lax.fori_loop(0, QUAD // 32, gate_rows, up_total)
+        rs3.post(s, lambda rows: gu[rows, :], lambda: w[1])
+        if s == 0:
+            for t in (1, 2):
+                gathers[1].ready(t)
+            tile(0, gzb, act, place.far)
+            to_x(2, 0, 2).start()
+            to_x(2, 0, 3).start()
+    for gather in gathers:
+        gather.end()
+    for peer in (place.core, place.ynb):
+        pl.semaphore_signal(gfree, inc=1, device_id=peer, device_id_type=MESH_ID)
+    n1_back = pltpu.make_async_copy(keep_h, n1a, ls.at[8])
+    n1_back.start()
+    outs[res_out].wait()
+    tok_back = pltpu.make_async_copy(tok_h, tok, ls.at[9])
+    tok_back.start()
+    small[pl.ds(8 + place.fs, 1), :] = up_total
+    add_x(2, 0, 1)
+    tile(1, n2, gu, place.far)
+    to_x(1, 1, 2).start()
+    to_x(1, 1, 3).start()
+    pl.semaphore_wait(gfree, 2)
+    ag3 = Gather(place, gzb, ags.at[5], agr.at[5])
+
+    def norm_rows(s, i, sums, values, gain, terms):
+        rows = _ds(SUB * s + 32 * i, 32, 32)
+        grad = terms.total(s, i, 32)
+        normed, reciprocal = _norm(values[rows, :].astype(F32))
+        scaled = grad * gain
+        back = (
+            scaled
+            - jnp.mean(scaled, axis=-1, keepdims=True)
+            - normed * jnp.mean(scaled * normed, axis=-1, keepdims=True)
+        ) * reciprocal
+        total = gy[rows, :] + back
+        gy[rows, :] = total
+        pair = (
+            sums[0] + jnp.sum(grad * normed, axis=0, keepdims=True),
+            sums[1] + jnp.sum(grad, axis=0, keepdims=True),
+        )
+        return total, pair
+
+    zero = jnp.zeros((1, D), F32)
+
+    def second_back(s, sums):
+        rs3.wait(s)
+
+        def rows_of(i, sums):
+            total, pair = norm_rows(s, i, sums[:2], mid, vecs[3:4, :], rs3)
+            low = total.astype(BF)
+            gzb[_ds(QUAD * s + 32 * i, 32, 32), :] = low
+            return pair + (sums[2] + jnp.sum(low.astype(F32), axis=0, keepdims=True),)
+
+        sums = lax.fori_loop(0, 4, rows_of, sums)
+        ag3.start(s)
+        return sums
+
+    gain2, shift2, outb = lax.fori_loop(0, 3, second_back, (zero, zero, zero))
+    small[2:3, :] = outb
+    small[3:4, :] = gain2
+    small[4:5, :] = shift2
+    tile(1, n2, gu, place.near)
+    to_x(1, 1, 1).start()
+    to_x(1, 1, 0).start()
+    add_x(2, 0, 2)
+    add_x(2, 0, 3)
+    rs3.end()
+    rs4 = Scatter(place, sb, rb, own, rss.at[4], rsr.at[4])
+
+    def attend_back(s, total):
+        ag3.pass_on(s)
+        ag3.ready(s)
+        acc[:, :W] = _nn(gzb[_ds(QUAD * s, QUAD, QUAD), :], wo[...])
+
+        def attend_rows(i, total):
+            rows = _ds(QUAD * s + SUB * i, SUB, SUB)
+            auxb = aux[rows, :]
+            qkb = qk[rows, :]
+            kqb = pltpu.roll(qkb.astype(F32), W, 1).astype(BF)
+            vb = v[rows, :]
+            gob = acc[_ds(SUB * i, SUB, SUB), :W].astype(BF)
+            keys = _stack(kqb, left)
+            scores = _nt(qkb, keys) * HD ** (-0.5)
+            probs = _softmax(scores, _allowed(auxb))
+            gprobs = _nt(gob, _stack(vb, side))
+            gscores = []
+            for h in range(HEADS_LOCAL):
+                gp = gprobs[:, 128 * h : 128 * h + 128]
+                delta = jnp.sum(gp * probs[h], axis=-1, keepdims=True)
+                gscores.append((probs[h] * (gp - delta)).astype(BF))
+            flat = jnp.concatenate(gscores, axis=1)
+            tall = jnp.concatenate(gscores, axis=0)
+            ptall = jnp.concatenate([p.astype(BF) for p in probs], axis=0)
+            gqk = (_nn(flat, keys) + _tn(tall, _stack(kqb, right))) * HD ** (-0.5)
+            gv = _tn(ptall, _stack(gob, side))
+            angle = _nn(auxb, tabs[...])
+            turned = (
+                gqk * angle[:, : 2 * W]
+                + pltpu.roll(gqk * angle[:, 4 * W :], 2 * W - 40, 1)
+                + pltpu.roll(gqk * angle[:, 2 * W : 4 * W], 40, 1)
+            )
+            low = jnp.concatenate([turned, gv], axis=1).astype(BF)
+            gu[rows, : 3 * W] = low
+            return total + jnp.sum(low.astype(F32), axis=0, keepdims=True)
+
+        total = lax.fori_loop(0, 4, attend_rows, total)
+        rs4.post(s, lambda rows: gu[rows, : 3 * W], lambda: w[0, :, : 3 * W])
+
+        @pl.when(s == 0)
+        def _():
+            add_x(1, 1, 2)
+
+        @pl.when(s == 1)
+        def _():
+            add_x(1, 1, 3)
+
+        return total
+
+    mix_total = lax.fori_loop(0, 3, attend_back, jnp.zeros((1, 3 * W), F32))
+    small[pl.ds(12 + place.fs, 1), : 3 * W] = mix_total
+
+    down_out = add_z(2, 0)
+    pl.semaphore_signal(xfree, inc=1, device_id=place.xnb, device_id_type=MESH_ID)
+    for peer in place.zn[1:]:
+        pl.semaphore_signal(zfree, inc=1, device_id=peer, device_id_type=MESH_ID)
+
+    for k in range(4):
+        to_x(2, 0, k).wait_send()
+    for k in range(1, 4):
+        to_z(2, 0, k).wait_send()
+    n1_back.wait()
+
+    def last_tile(half):
+        rows = _ds(HALF * half, HALF, 128)
+        gb[0, rows, : 3 * W] = _tn(n1a[:, rows], gu[:, : 3 * W]).astype(BF)
+        gb[0, rows, 3 * W :] = _tn(gzb[:, rows], o[...]).astype(BF)
+
+    last_tile(place.far)
+    pl.semaphore_wait(xfree, 1)
+    to_x(0, 0, 2).start()
+    to_x(0, 0, 3).start()
+    last_tile(place.near)
+    to_x(0, 0, 1).start()
+    to_x(0, 0, 0).start()
+    add_x(1, 1, 1)
+
+    tok_back.wait()
+
+    def first_back(s, sums):
+        rs4.wait(s)
+        return lax.fori_loop(0, 4, lambda i, t: norm_rows(s, i, t, tok, vecs[0:1, :], rs4)[1], sums)
+
+    gain1, shift1 = lax.fori_loop(0, 3, first_back, (zero, zero))
+    out(gy, gtok_h)
+    small[0:1, :] = gain1
+    small[1:2, :] = shift1
+
+    hops = [
+        _send(stage.at[i], came.at[i], ss.at[i], sr.at[i], peer)
+        for i, peer in enumerate((place.core, place.ynb, place.xnb, place.zn[1], place.zn[2]))
+    ]
+    for hop_ in vector_hops:
+        hop_.wait_send()
+    stage[0] = small[...]
+    hops[0].start()
+    pl.semaphore_wait(zfree, 3)
+    outs[down_out].wait()
+
+    def next_hop(i):
+        hops[i].wait_recv()
+        total = stage[i] + came[i]
+        if i < 4:
+            stage[i + 1] = total
+            hops[i + 1].start()
+        else:
+            small_o[...] = total
+            loss_o[...] = jnp.sum(total[6:7, :], axis=-1, keepdims=True) / (real_count * D)
+
+    add_x(0, 0, 2)
+    next_hop(0)
+    up_out = add_z(1, 1)
+    next_hop(1)
+    add_x(0, 0, 3)
+    next_hop(2)
+    add_x(0, 0, 1)
+    next_hop(3)
+    next_hop(4)
+    outs[up_out].wait()
+    add_z(0, 0)
+
+    for piece in range(4):
+        sent(piece)
+    agx.end()
+    ag2.end()
+    ag3.end()
+    rs4.end()
+    for hop_ in count_hops + hops:
+        hop_.wait_send()
+    for chunk, slot in ((1, 1), (0, 0)):
+        for k in range(4):
+            to_x(chunk, slot, k).wait_send()
+        for k in range(1, 4):
+            to_z(chunk, slot, k).wait_send()
+    for i, copy in enumerate(outs):
+        if i not in (n1_kept, res_out, down_out, up_out):
+            copy.wait()
+
+
+TOTAL = [0]
+
+
+def layer_call(*operands):
+    any_, vm = pl.ANY, pltpu.VMEM
+    outs = [
+        ((R, D), BF, any_),
+        ((R, D), F32, any_),
+        ((3, BLK, D), F32, any_),
+        ((16, D), F32, vm),
+        ((1, 1), F32, vm),
+        ((G, D), BF, any_),
+    ]
+    dma = pltpu.SemaphoreType.DMA
+    scratch = [
+        vm((R, D), BF),
+        vm((G, 128), BF),
+        vm((3, D, D), BF),
+        vm((D, W), BF),
+        vm((G, D), BF),
+        vm((G, D), BF),
+        vm((G, F), BF),
+        vm((G, D), BF),
+        vm((G, 2 * W), BF),
+        vm((G, W), BF),
+        vm((G, W), BF),
+        vm((QUAD, D), F32),
+        vm((R, D), F32),
+        vm((R, D), F32),
+        vm((R, D), F32),
+        vm((5, SUB, D), BF),
+        vm((3, 3, SUB, D), BF),
+        vm((2, D, D), BF),
+        vm((2, 4, BLK, D), BF),
+        vm((2, 3, BLK, D), BF),
+        vm((BLK, D), F32),
+        vm((8, D), F32),
+        vm((3, 8, 128), F32),
+        vm((3, 8, 128), F32),
+        vm((16, D), F32),
+        vm((5, 16, D), F32),
+        vm((5, 16, D), F32),
+        dma((4, 15)),
+        dma((4, 8)),
+        dma((6, 9)),
+        dma((6, 9)),
+        dma((5, 9)),
+        dma((5, 9)),
+        dma((3,)),
+        dma((3,)),
+        dma((3,)),
+        dma((3,)),
+        dma((3, 4)),
+        dma((3, 4)),
+        dma((3, 3)),
+        dma((3, 3)),
+        dma((5,)),
+        dma((5,)),
+        dma((10,)),
+        dma((8,)),
+        pltpu.SemaphoreType.REGULAR,
+        pltpu.SemaphoreType.REGULAR,
+        pltpu.SemaphoreType.REGULAR,
+    ]
+    ins = [any_] * 6 + [vm] * 2
+    return pl.pallas_call(
+        layer_kernel,
+        out_shape=[jax.ShapeDtypeStruct(shape, dtype) for shape, dtype, _ in outs],
+        in_specs=[pl.BlockSpec(memory_space=space) for space in ins],
+        out_specs=[pl.BlockSpec(memory_space=space) for _, _, space in outs],
+        scratch_shapes=scratch,
+        compiler_params=pltpu.CompilerParams(
+            collective_id=1, has_side_effects=True, vmem_limit_bytes=64 << 20
+        ),
+        name="layer",
+    )(*operands)
+
+
+def turn_tables():
+    import ml_dtypes
+
+    quarter = HD // 4
+    frequency = (1.0 / np.float32(10000.0) ** (np.arange(quarter, dtype=np.float32) * 4.0 / HD)).astype(np.float32)
+    angle = (np.arange(16, dtype=np.float32)[:, None] * frequency[None, :]).astype(np.float32)
+    cosine, sine = np.cos(angle.astype(np.float64)), np.sin(angle.astype(np.float64))
+    zero = np.zeros_like(cosine)
+
+    def head(first, second):
+        top = np.concatenate([first, zero, second, zero], axis=1)
+        low = np.concatenate([zero, first, zero, second], axis=1)
+        return np.tile(np.concatenate([top, low], axis=0), (1, 2 * HEADS_LOCAL))
+
+    full = np.concatenate([head(cosine, cosine), head(-sine, zero), head(zero, sine)], axis=1).astype(np.float32)
+    terms = []
+    rest = full
+    for _ in range(3):
+        term = rest.astype(ml_dtypes.bfloat16)
+        terms.append(term)
+        rest = rest - term.astype(np.float32)
+    terms.append(np.zeros((32, full.shape[1]), ml_dtypes.bfloat16))
+    return jnp.asarray(np.concatenate(terms, axis=0))
+
+
+def row_marks(picture, places, validity):
+    spots = jnp.arange(16, dtype=jnp.int32)
+    row_spot = places[:, 0:1] == spots
+    col_spot = places[:, 1:2] == spots
+    pictures = picture.reshape(-1, ROW_PATCHES)
+    change = (pictures[:, 1:] != pictures[:, :-1]).astype(BF)
+    change = jnp.pad(change, ((0, 0), (1, 0)))
+    upto = jnp.triu(jnp.ones((ROW_PATCHES, ROW_PATCHES), BF))
+    rank = jnp.dot(change, upto, preferred_element_type=F32).reshape(-1, 1)
+    ranks = rank == jnp.arange(8, dtype=F32)
+    once = jnp.concatenate([row_spot, col_spot], axis=1)
+    return jnp.concatenate(
+        [once, once, once, ranks, (validity > 0)[:, None], jnp.zeros((picture.shape[0], 23), bool)], axis=1
+    ).astype(BF)
+
+
+def on_device_fast(
+    tokens,
+    teacher,
+    picture,
+    places,
+    validity,
+    first_gain,
+    first_shift,
+    mixer_weight,
+    mixer_bias,
+    output_weight,
+    output_bias,
+    second_gain,
+    second_shift,
+    upward_weight,
+    upward_bias,
+    downward_weight,
+    downward_bias,
+):
+    member = lax.axis_index("fsdp")
+    data_index = lax.axis_index("dp")
+    data_ways = lax.axis_size("dp")
+    TOTAL[0] = float(tokens.shape[0] * data_ways * lax.axis_size("fsdp"))
+    marks = row_marks(picture, places, validity)
+    vectors = (first_gain, first_shift, output_bias, second_gain, second_shift, downward_bias)
+    spots = jnp.zeros((6, D), F32)
+    spots = lax.dynamic_update_slice(spots, jnp.stack(vectors).astype(F32), (0, BLK * data_index))
+    up_all = lax.dynamic_update_slice(jnp.zeros((FF,), F32), upward_bias.astype(F32), (640 * data_index,))
+    up_piece = lax.dynamic_slice_in_dim(up_all.reshape(4, F), member, 1, 0)
+    mix_all = lax.dynamic_update_slice(jnp.zeros((3 * D,), F32), mixer_bias.astype(F32), (480 * data_index,))
+    mix_piece = lax.dynamic_slice_in_dim(mix_all.reshape(3, 4, W), member, 1, 1).reshape(1, 3 * W)
+    sv = jnp.concatenate([spots, up_piece, jnp.pad(mix_piece, ((0, 0), (0, D - 3 * W)))], axis=0)
+    wa = jnp.concatenate([mixer_weight.reshape(BLK, 3 * W), output_weight.T], axis=1)
+    tabs = turn_tables()
+    res, gtok, gw, small, loss, _ = layer_call(
+        tokens, teacher, marks, wa, upward_weight, downward_weight.T, sv, tabs
+    )
+    pieces = [own_slice(small[i], data_index, data_ways) for i in range(6)]
+    up_bias = own_slice(small[8:12].reshape(FF), data_index, data_ways)
+    mixed = small[12:16, : 3 * W].reshape(4, 3, W).transpose(1, 0, 2).reshape(3 * D)
+    return (
+        res,
+        loss.reshape(()),
+        gtok,
+        pieces[0],
+        pieces[1],
+        gw[0, :, : 3 * W].reshape(BLK, 3, W),
+        own_slice(mixed[: 2 * D], data_index, data_ways),
+        own_slice(mixed[2 * D :], data_index, data_ways),
+        gw[0, :, 3 * W :].T,
+        pieces[2],
+        pieces[3],
+        pieces[4],
+        gw[1],
+        up_bias,
+        gw[2].T,
+        pieces[5],
+    )
+
+
 def solution(mesh):
+    fast = mesh.shape["dp"] == 8 and mesh.shape["fsdp"] == 4
     return jax.shard_map(
-        on_device,
+        on_device_fast if fast else on_device,
         mesh=mesh,
         in_specs=(
             P(("dp", "fsdp"), None),

time: 1220 us -> 353 us (0.29)
  waiting for transfers between devices: 614 us -> 0 us
  Pallas kernels: 0 us -> 314 us
  blocking collectives: 232 us -> 0 us
  matrix products: 145 us -> 0.2 us
  other arithmetic: 87.7 us -> 5.54 us
  local copies, waits for them, and re-layouts: 106 us -> 26.6 us
  between operations: 24 us -> 2.84 us
    reduce_scatter x16 -> x0, waiting for transfers between devices: 371 us -> none  [the longest x3 85.1 us: on_device(): lax.psum_scatter(jnp.einsum('re,de->rd', grad_mixed, mixer_flat, preferre...]
    pallas_call x0 -> x1, Pallas kernels: none -> 314 us  [layer_call(): pl.pallas_call(layer_kernel, out_shape=[jax.ShapeDtypeStruct(shape, dtype...]
    all_gather x15 -> x0, waiting for transfers between devices: 240 us -> none  [the longest x1 58.5 us: on_device(): lax.all_gather(downward_weight, 'dp', axis=1, tiled=True)]
    dot_general x54 -> x1, matrix products: 145 us -> 0.2 us  [row_marks(): rank = jnp.dot(change, upto, preferred_element_type=F32).reshape(-1, 1)]
    all_gather x11 -> x0, blocking collectives: 109 us -> none  [the longest x1 32.7 us: on_device(): lax.all_gather(output_weight, 'dp', axis=1, tiled=True)]
    psum x2 -> x0, blocking collectives: 82.4 us -> none  [the longest x1 43.1 us: on_device(): lax.psum((small_sums[0], small_sums[1], small_sums[2], small_sums[3], sma...]
    unnamed x1 -> x0, blocking collectives: 40.7 us -> none
    reduce_sum x20 -> x0, other arithmetic: 32.2 us -> none  [the longest x3 9.69 us: on_device(): out_bias_term = jnp.sum(grad_branch.astype(jnp.float32), axis=0)]
  transfers between devices with their start and end apart: 31 -> 0, of which waited for: 25 -> 0; matrix products, arithmetic and copies ran while one was open for 22% -> 0% of each run, Pallas kernels for 0% -> 0%
where the time goes in v2:
time: 353 us; the launch traced here: 349 us
  Pallas kernels  314 us (89%)
  local copies, waits for them, and re-layouts  26.6 us (8%)
  other arithmetic  5.54 us (2%)
    pallas_call x1, Pallas kernels, layer_call(): pl.pallas_call(layer_kernel, out_shape=[jax.ShapeDtypeStruct(shape, dtype...  314 us

profile of v2, /device:TPU:0, one launch (start us, length us, event | category | flops | bytes accessed | tf_op | source)
XLA Modules:
  0.0 348.8 jit_solution(512686818264141323)
XLA Ops:
  0.6 0.0 copy-start.1
  0.7 0.8 slice_compare_fusion
  1.5 0.7 broadcast_compare_fusion
  2.2 0.2 convolution_bitcast_fusion
  2.4 0.7 stack.21
  3.0 0.7 stack.22
  3.7 0.7 stack.23
  4.4 0.7 stack.24
  5.0 0.7 stack.25
  5.7 0.7 stack.26
  6.4 0.8 slice_reduce_fusion.1
  7.2 0.8 convert_dynamic-update-slice_fusion.1
  8.0 0.1 reshape.70
  8.1 0.1 reshape.71
  8.2 0.8 convert_dynamic-update-slice_fusion
  9.0 0.3 dynamic_update_slice.9
  9.3 0.6 select_maximum_fusion.sv
  9.9 0.1 iota_compare_fusion
  10.0 0.1 broadcast_in_dim.32
  10.2 0.2 iota_compare_fusion.1
  10.4 0.5 concatenate.11
  10.9 0.7 convert_element_type.17.aux_h
  11.6 1.2 copy.37
  12.8 0.3 reshape.68
  13.1 0.0 copy-done.1
  13.1 0.9 pad_maximum_fusion.wa_h
  14.0 313.7 %layer.1 = (bf16[384,1280]{1,0:T(8,128)(2,1)}, f32[384,1280]{1,0:T(8,128)}, f32[3,160,1280]{2,1,0:T(8,128)}, f32[16,1280]{1,0:T(8,128)}, f32[1,1]{1,0:T(1,128)}, /*index=5*/bf16[1536,1280]{1,0:T(8,128)(2,1)}) custom-call(bf16[384,1280]{1,0:T(8,128)(2,1)} %tok_h.1, bf16[384,1280]{1,0:T(8,128)(2,1)} %teach_h.1, bf16[384,128]{1,0:T(8,128)(2,1)} %convert_element_type.17.aux_h, ...), custom_call_target="tpu_custom_call" | custom-call | tf_op jit(solution)/shard_map/layer/pallas_call | solution.py:1236
  327.7 0.8 slice.67
  328.5 0.1 reshape.73
  328.6 0.1 slice.69
  328.7 0.7 dynamic_slice.51
  329.3 0.1 slice.71
  329.4 0.6 dynamic_slice.52
  330.1 0.8 slice.77
  330.8 1.1 fusion.9
  331.9 0.6 constant_dynamic-slice_fusion
  332.6 0.7 dynamic_slice.59
  333.3 0.6 constant_dynamic-slice_fusion.1
  333.9 0.6 constant_dynamic-slice_fusion.2
  334.5 0.6 constant_dynamic-slice_fusion.3
  335.2 0.6 constant_dynamic-slice_fusion.4
  335.8 0.6 constant_dynamic-slice_fusion.5
  336.4 1.8 slice_bitcast_fusion.2
  338.2 1.1 slice.66
  339.3 2.7 slice_bitcast_fusion
  342.0 0.4 reshape_squeeze.3
  342.4 0.0 copy-start
  342.4 0.9 copy.39
  343.3 2.2 copy.46
  346.2 0.0 copy-done
  346.2 1.3 copy.48
  (14 shorter events, 0.2 us)
Async XLA Ops:
  0.6 12.5 %copy-start.1 = (bf16[320,160]{0,1:T(8,128)(2,1)S(1)}, bf16[320,160]{0,1:T(8,128)(2,1)}, u32[]{:S(2)}) copy-start(bf16[320,160]{0,1:T(8,128)(2,1)} %param.27) | copy-start | bytes 307204
  342.4 3.8 %copy-start = (f32[384,1280]{1,0:T(8,128)S(1)}, f32[384,1280]{1,0:T(8,128)}, u32[]{:S(2)}) copy-start(f32[384,1280]{1,0:T(8,128)} %get-tuple-element.88) | copy-start | bytes 5898244
